TPU v7x, 32 devices: a whole 2x2x4 slice. The times are simulated.
32 devices in a mesh: dp: 8 (over y, x, core), tensor: 4 (over z).
Axes of the slice: x: 2, y: 2, z: 4, core: 2. Of those that a mesh axis runs over, the one named last changes fastest.
Arguments:
- x_in: float32 [1024, 1024], P(('dp', 'tensor')), may hold values from -6 to 6
- seq_lengths: int32 [8, 8], P('dp'), may hold values from 1 to 64, 128 in all within a row
- ln1_gain: float32 [2, 1024], P(None, ('dp', 'tensor')), may hold values from 0.5 to 1.5
- ln1_bias: float32 [2, 1024], P(None, ('dp', 'tensor')), may hold values from -3 to 3
- ln2_gain: float32 [2, 1024], P(None, ('dp', 'tensor')), may hold values from 0.5 to 1.5
- ln2_bias: float32 [2, 1024], P(None, ('dp', 'tensor')), may hold values from -3 to 3
- res_bias: float32 [2, 1024], P(None, ('dp', 'tensor')), may hold values from -3 to 3
- w_qkv: bfloat16 [2, 1024, 3, 1024], P(None, 'dp', None, 'tensor'), may hold values from -1 to 1
- b_qkv: float32 [2, 3, 1024], P(None, None, ('tensor', 'dp')), may hold values from -3 to 3
- w_out: bfloat16 [2, 1024, 1024], P(None, 'tensor', 'dp'), may hold values from -0.75 to 0.75
- w_fc: bfloat16 [2, 1024, 4096], P(None, 'dp', 'tensor'), may hold values from -0.1875 to 0.1875
- b_fc: float32 [2, 4096], P(None, ('tensor', 'dp')), may hold values from -3 to 3
- w_proj: bfloat16 [2, 4096, 1024], P(None, 'tensor', 'dp'), may hold values from -0.09375 to 0.09375
- grad_out: float32 [1024, 1024], P(('dp', 'tensor')), may hold values from -6 to 6
Outputs:
- y_out: float32 [1024, 1024], P(('dp', 'tensor'))
- grad_x: float32 [1024, 1024], P(('dp', 'tensor'))
- grad_ln1_gain: float32 [2, 1024], P(None, ('dp', 'tensor'))
- grad_ln1_bias: float32 [2, 1024], P(None, ('dp', 'tensor'))
- grad_ln2_gain: float32 [2, 1024], P(None, ('dp', 'tensor'))
- grad_ln2_bias: float32 [2, 1024], P(None, ('dp', 'tensor'))
- grad_res_bias: float32 [2, 1024], P(None, ('dp', 'tensor'))
- grad_w_qkv: float32 [2, 1024, 3, 1024], P(None, 'dp', None, 'tensor')
- grad_b_qkv: float32 [2, 3, 1024], P(None, None, ('tensor', 'dp'))
- grad_w_out: float32 [2, 1024, 1024], P(None, 'tensor', 'dp')
- grad_w_fc: float32 [2, 1024, 4096], P(None, 'dp', 'tensor')
- grad_b_fc: float32 [2, 4096], P(None, ('tensor', 'dp'))
- grad_w_proj: float32 [2, 4096, 1024], P(None, 'tensor', 'dp')
Inputs may be any that keep to these rules, and one draw needn't show every extreme that they name: `seq_lengths`: in every row the lengths sum to 128 and the largest is exactly 64.
All inputs are finite; a program needn't handle non-finite values.
Results may differ from a plain program's by a relative error of at most 0.035.
Values may be sent and summed in bfloat16 or wider, within the bound.
A program may use at most 128 MiB of HBM per device.

v0:
```python
import jax
import jax.numpy as jnp
from jax import lax
from jax.sharding import PartitionSpec as P

HD = 64
ROT = 16


EPS = 1e-05
NEG_FILL = -1e30


def layer_norm(values, gain_vec, bias_vec):
    average = jnp.mean(values, axis=-1, keepdims=True)
    centred = values - average
    variance = jnp.mean(centred * centred, axis=-1, keepdims=True)
    return centred * lax.rsqrt(variance + EPS) * gain_vec + bias_vec


def gelu_exact(values):
    return 0.5 * values * (1.0 + jax.scipy.special.erf(values * 0.7071067811865476))


def gelu_slope(values):
    normal_cdf = 0.5 * (1.0 + jax.scipy.special.erf(values * 0.7071067811865476))
    return normal_cdf + values * jnp.exp(-0.5 * values * values) * 0.3989422804014327


def group_layout(seq_len, total_rows):
    ends = jnp.cumsum(seq_len)
    starts = ends - seq_len
    row_ids = jnp.arange(total_rows, dtype=jnp.int32)
    member = (row_ids[:, None] >= starts[None, :]) & (row_ids[:, None] < ends[None, :])
    seq_index = jnp.arange(seq_len.shape[0], dtype=jnp.int32)
    seq_ids = jnp.sum(jnp.where(member, seq_index[None, :], 0), axis=1)
    row_start = jnp.sum(jnp.where(member, starts[None, :], 0), axis=1)
    return (seq_ids, row_ids - row_start, row_ids)


def rotary_tables(positions):
    half_rot = ROT // 2
    freq_ids = jnp.arange(half_rot, dtype=jnp.float32)
    inverse = jnp.power(10000.0, -2.0 * freq_ids / ROT)
    angles = positions.astype(jnp.float32)[:, None] * inverse[None, :]
    return (jnp.cos(angles), jnp.sin(angles))


def rotate(vectors, cos_tab, sin_tab, direction_sign):
    half_rot = ROT // 2
    lower_half = vectors[..., :half_rot]
    upper_half = vectors[..., half_rot:ROT]
    cos_b = cos_tab[:, None, :]
    sin_b = sin_tab[:, None, :]
    new_lower = lower_half * cos_b - direction_sign * upper_half * sin_b
    new_upper = upper_half * cos_b + direction_sign * lower_half * sin_b
    return jnp.concatenate([new_lower, new_upper, vectors[..., ROT:]], axis=-1)


def masked_block(q_blk, keys, q_seq, q_row, seq_ids, row_ids):
    scores = jnp.einsum("qhd,khd->hqk", q_blk, keys, preferred_element_type=jnp.float32) * HD ** (
        -0.5
    )
    allowed = (q_seq[:, None] == seq_ids[None, :]) & (row_ids[None, :] <= q_row[:, None])
    return jnp.where(allowed[None], scores, NEG_FILL)


def attention_forward(queries, keys, values, seq_ids, row_ids):
    total_rows, heads_here, head_dim = queries.shape
    block_rows = min(512, total_rows)
    blocks = total_rows // block_rows

    def one_block(inputs):
        q_blk, q_seq, q_row = inputs
        scores = masked_block(q_blk, keys, q_seq, q_row, seq_ids, row_ids)
        top_val = jnp.max(scores, axis=-1, keepdims=True)
        exponent_terms = jnp.exp(scores - top_val)
        totals = jnp.sum(exponent_terms, axis=-1, keepdims=True)
        attn_probs = (exponent_terms / totals).astype(jnp.bfloat16)
        context = jnp.einsum(
            "hqk,khd->qhd", attn_probs, values, preferred_element_type=jnp.float32
        ).astype(jnp.bfloat16)
        return (context, (top_val + jnp.log(totals))[..., 0])

    contexts, log_totals = lax.map(
        one_block,
        (
            queries.reshape(blocks, block_rows, heads_here, head_dim),
            seq_ids.reshape(blocks, block_rows),
            row_ids.reshape(blocks, block_rows),
        ),
    )
    return (contexts.reshape(total_rows, heads_here, head_dim), log_totals)


def attention_backward(queries, keys, values, contexts, d_context, log_totals, seq_ids, row_ids):
    total_rows, heads_here, head_dim = queries.shape
    block_rows = min(512, total_rows)
    blocks = total_rows // block_rows

    def one_block(carry, inputs):
        d_keys, d_values = carry
        q_blk, c_blk, dc_blk, lse_blk, q_seq, q_row = inputs
        scores = masked_block(q_blk, keys, q_seq, q_row, seq_ids, row_ids)
        probs_full = jnp.exp(scores - lse_blk[..., None])
        d_probs = jnp.einsum("qhd,khd->hqk", dc_blk, values, preferred_element_type=jnp.float32)
        delta = jnp.sum(dc_blk.astype(jnp.float32) * c_blk.astype(jnp.float32), axis=-1)
        d_scores = probs_full * (d_probs - jnp.transpose(delta)[:, :, None])
        d_scaled = (d_scores * HD ** (-0.5)).astype(jnp.bfloat16)
        d_q = jnp.einsum("hqk,khd->qhd", d_scaled, keys, preferred_element_type=jnp.float32)
        d_keys = d_keys + jnp.einsum(
            "hqk,qhd->khd", d_scaled, q_blk, preferred_element_type=jnp.float32
        )
        d_values = d_values + jnp.einsum(
            "hqk,qhd->khd",
            probs_full.astype(jnp.bfloat16),
            dc_blk,
            preferred_element_type=jnp.float32,
        )
        return ((d_keys, d_values), d_q)

    zero_keys = jnp.zeros(keys.shape, jnp.float32)
    shape_blk = (blocks, block_rows, heads_here, head_dim)
    carry_out, d_queries = lax.scan(
        one_block,
        (zero_keys, zero_keys),
        (
            queries.reshape(shape_blk),
            contexts.reshape(shape_blk),
            d_context.reshape(shape_blk),
            log_totals,
            seq_ids.reshape(blocks, block_rows),
            row_ids.reshape(blocks, block_rows),
        ),
    )
    return (d_queries.reshape(total_rows, heads_here, head_dim), carry_out[0], carry_out[1])


def stack_layers(per_layer, member_idx):
    return jnp.stack([entry[member_idx] for entry in per_layer])


def per_device(
    x_in,
    seq_lengths,
    ln1_gain,
    ln1_bias,
    ln2_gain,
    ln2_bias,
    res_bias,
    w_qkv,
    b_qkv,
    w_out,
    w_fc,
    b_fc,
    w_proj,
    grad_out,
):
    tensor_size = lax.axis_size("tensor")
    my_rows = x_in.shape[0]
    group_rows = my_rows * tensor_size
    layer_count = w_qkv.shape[0]
    heads_here = w_qkv.shape[3] // HD
    gain_one, bias_one, gain_two, bias_two, out_bias = (
        lax.all_gather(ln1_gain, ("dp", "tensor"), axis=1, tiled=True),
        lax.all_gather(ln1_bias, ("dp", "tensor"), axis=1, tiled=True),
        lax.all_gather(ln2_gain, ("dp", "tensor"), axis=1, tiled=True),
        lax.all_gather(ln2_bias, ("dp", "tensor"), axis=1, tiled=True),
        lax.all_gather(res_bias, ("dp", "tensor"), axis=1, tiled=True),
    )
    seq_ids, positions, row_ids = group_layout(seq_lengths[0], group_rows)
    cos_tab, sin_tab = rotary_tables(positions)
    resid = x_in
    saved = []
    kept_weights = []
    for layer_idx in range(layer_count):
        weights = (
            lax.all_gather(w_qkv[layer_idx], "dp", axis=0, tiled=True),
            lax.all_gather(b_qkv[layer_idx].astype(jnp.bfloat16), "dp", axis=1, tiled=True).astype(
                jnp.float32
            ),
            lax.all_gather(w_out[layer_idx], "dp", axis=1, tiled=True),
            lax.all_gather(w_fc[layer_idx], "dp", axis=0, tiled=True),
            lax.all_gather(b_fc[layer_idx].astype(jnp.bfloat16), "dp", axis=0, tiled=True).astype(
                jnp.float32
            ),
            lax.all_gather(w_proj[layer_idx], "dp", axis=1, tiled=True),
        )
        qkv_mat, qkv_vec, out_mat, fc_mat, fc_vec, proj_mat = weights
        normed_pair = jnp.stack(
            [
                layer_norm(resid, gain_one[layer_idx], bias_one[layer_idx]),
                layer_norm(resid, gain_two[layer_idx], bias_two[layer_idx]),
            ]
        ).astype(jnp.bfloat16)
        rows_pair = lax.all_gather(normed_pair, "tensor", axis=1, tiled=True)
        projected = (
            jnp.dot(
                rows_pair[0],
                qkv_mat.reshape(qkv_mat.shape[0], -1),
                preferred_element_type=jnp.float32,
            ).reshape(group_rows, 3, -1)
            + qkv_vec[None]
        )
        split_heads = projected.reshape(group_rows, 3, heads_here, HD)
        queries = rotate(split_heads[:, 0], cos_tab, sin_tab, 1.0).astype(jnp.bfloat16)
        keys = rotate(split_heads[:, 1], cos_tab, sin_tab, 1.0).astype(jnp.bfloat16)
        values = split_heads[:, 2].astype(jnp.bfloat16)
        contexts, log_totals = attention_forward(queries, keys, values, seq_ids, row_ids)
        hidden_pre = jnp.dot(rows_pair[1], fc_mat, preferred_element_type=jnp.float32) + fc_vec
        activated = gelu_exact(hidden_pre).astype(jnp.bfloat16)
        flat_context = contexts.reshape(group_rows, -1)
        branch = lax.psum_scatter(
            (
                jnp.dot(flat_context, out_mat, preferred_element_type=jnp.float32)
                + jnp.dot(activated, proj_mat, preferred_element_type=jnp.float32)
            ).astype(jnp.bfloat16),
            "tensor",
            scatter_dimension=0,
            tiled=True,
        ).astype(jnp.float32)
        saved.append(
            (resid, rows_pair, queries, keys, values, contexts, log_totals, hidden_pre, activated)
        )
        kept_weights.append(weights)
        resid = resid + branch + out_bias[layer_idx]
    d_resid = grad_out
    grads_list = [None] * layer_count
    for layer_idx in reversed(range(layer_count)):
        (
            layer_input,
            rows_pair,
            queries,
            keys,
            values,
            contexts,
            log_totals,
            hidden_pre,
            activated,
        ) = saved[layer_idx]
        qkv_mat, qkv_vec, out_mat, fc_mat, fc_vec, proj_mat = (
            lax.all_gather(w_qkv[layer_idx], "dp", axis=0, tiled=True),
            lax.all_gather(b_qkv[layer_idx].astype(jnp.bfloat16), "dp", axis=1, tiled=True).astype(
                jnp.float32
            ),
            lax.all_gather(w_out[layer_idx], "dp", axis=1, tiled=True),
            lax.all_gather(w_fc[layer_idx], "dp", axis=0, tiled=True),
            lax.all_gather(b_fc[layer_idx].astype(jnp.bfloat16), "dp", axis=0, tiled=True).astype(
                jnp.float32
            ),
            lax.all_gather(w_proj[layer_idx], "dp", axis=1, tiled=True),
        )
        out_bias_grad = jnp.sum(d_resid, axis=0)
        d_rows = lax.all_gather(d_resid.astype(jnp.bfloat16), "tensor", axis=0, tiled=True)
        flat_context = contexts.reshape(group_rows, -1)
        d_context = jnp.dot(d_rows, out_mat.T, preferred_element_type=jnp.float32).astype(
            jnp.bfloat16
        )
        grad_out_mat = jnp.dot(flat_context.T, d_rows, preferred_element_type=jnp.float32)
        d_act = jnp.dot(d_rows, proj_mat.T, preferred_element_type=jnp.float32)
        grad_proj_mat = jnp.dot(activated.T, d_rows, preferred_element_type=jnp.float32)
        d_pre = d_act * gelu_slope(hidden_pre)
        grad_fc_vec = jnp.sum(d_pre, axis=0)
        d_pre_b = d_pre.astype(jnp.bfloat16)
        grad_fc_mat = jnp.dot(rows_pair[1].T, d_pre_b, preferred_element_type=jnp.float32)
        d_queries, d_keys, d_values = attention_backward(
            queries,
            keys,
            values,
            contexts,
            d_context.reshape(group_rows, heads_here, HD),
            log_totals,
            seq_ids,
            row_ids,
        )
        d_queries = rotate(d_queries, cos_tab, sin_tab, -1.0)
        d_keys = rotate(d_keys, cos_tab, sin_tab, -1.0)
        d_projected = jnp.stack([d_queries, d_keys, d_values], axis=1).reshape(group_rows, 3, -1)
        grad_qkv_vec = jnp.sum(d_projected, axis=0)
        flat_dqkv = d_projected.astype(jnp.bfloat16).reshape(group_rows, -1)
        grad_qkv_mat = jnp.dot(
            rows_pair[0].T, flat_dqkv, preferred_element_type=jnp.float32
        ).reshape(qkv_mat.shape)
        flat_qkv = qkv_mat.reshape(qkv_mat.shape[0], -1)
        d_normed = lax.psum_scatter(
            jnp.stack(
                [
                    jnp.dot(flat_dqkv, flat_qkv.T, preferred_element_type=jnp.float32),
                    jnp.dot(d_pre_b, fc_mat.T, preferred_element_type=jnp.float32),
                ],
                axis=1,
            ).astype(jnp.bfloat16),
            "tensor",
            scatter_dimension=0,
            tiled=True,
        ).astype(jnp.float32)
        unused_one, back_one = jax.vjp(
            layer_norm, layer_input, gain_one[layer_idx], bias_one[layer_idx]
        )
        d_res_one, grad_gain_one, grad_bias_one = back_one(d_normed[:, 0])
        unused_two, back_two = jax.vjp(
            layer_norm, layer_input, gain_two[layer_idx], bias_two[layer_idx]
        )
        d_res_two, grad_gain_two, grad_bias_two = back_two(d_normed[:, 1])
        weight_grads = tuple(
            (
                lax.psum_scatter(
                    grad_qkv_mat.astype(jnp.bfloat16), "dp", scatter_dimension=0, tiled=True
                ).astype(jnp.float32),
                lax.psum_scatter(
                    grad_qkv_vec.astype(jnp.bfloat16), "dp", scatter_dimension=1, tiled=True
                ).astype(jnp.float32),
                lax.psum_scatter(
                    grad_out_mat.astype(jnp.bfloat16), "dp", scatter_dimension=1, tiled=True
                ).astype(jnp.float32),
                lax.psum_scatter(
                    grad_fc_mat.astype(jnp.bfloat16), "dp", scatter_dimension=0, tiled=True
                ).astype(jnp.float32),
                lax.psum_scatter(
                    grad_fc_vec.astype(jnp.bfloat16), "dp", scatter_dimension=0, tiled=True
                ).astype(jnp.float32),
                lax.psum_scatter(
                    grad_proj_mat.astype(jnp.bfloat16), "dp", scatter_dimension=1, tiled=True
                ).astype(jnp.float32),
            )
        )
        grads_list[layer_idx] = weight_grads + (
            grad_gain_one,
            grad_bias_one,
            grad_gain_two,
            grad_bias_two,
            out_bias_grad,
        )
        d_resid = d_resid + d_res_one + d_res_two
    gain_one_grad = stack_layers(grads_list, 6)
    bias_one_grad = stack_layers(grads_list, 7)
    gain_two_grad = stack_layers(grads_list, 8)
    bias_two_grad = stack_layers(grads_list, 9)
    res_bias_grad = stack_layers(grads_list, 10)
    small_grads = (
        lax.psum_scatter(gain_one_grad, ("dp", "tensor"), scatter_dimension=1, tiled=True),
        lax.psum_scatter(bias_one_grad, ("dp", "tensor"), scatter_dimension=1, tiled=True),
        lax.psum_scatter(gain_two_grad, ("dp", "tensor"), scatter_dimension=1, tiled=True),
        lax.psum_scatter(bias_two_grad, ("dp", "tensor"), scatter_dimension=1, tiled=True),
        lax.psum_scatter(res_bias_grad, ("dp", "tensor"), scatter_dimension=1, tiled=True),
    )
    stacked_grads = tuple((stack_layers(grads_list, member_idx) for member_idx in range(6)))
    return (
        resid,
        d_resid,
        small_grads[0],
        small_grads[1],
        small_grads[2],
        small_grads[3],
        small_grads[4],
        stacked_grads[0],
        stacked_grads[1],
        stacked_grads[2],
        stacked_grads[3],
        stacked_grads[4],
        stacked_grads[5],
    )


def solution(mesh):
    in_specs = (
        P(("dp", "tensor"), None),
        P("dp", None),
        P(None, ("dp", "tensor")),
        P(None, ("dp", "tensor")),
        P(None, ("dp", "tensor")),
        P(None, ("dp", "tensor")),
        P(None, ("dp", "tensor")),
        P(None, "dp", None, "tensor"),
        P(None, None, ("tensor", "dp")),
        P(None, "tensor", "dp"),
        P(None, "dp", "tensor"),
        P(None, ("tensor", "dp")),
        P(None, "tensor", "dp"),
        P(("dp", "tensor"), None),
    )
    out_specs = (
        P(("dp", "tensor"), None),
        P(("dp", "tensor"), None),
        P(None, ("dp", "tensor")),
        P(None, ("dp", "tensor")),
        P(None, ("dp", "tensor")),
        P(None, ("dp", "tensor")),
        P(None, ("dp", "tensor")),
        P(None, "dp", None, "tensor"),
        P(None, None, ("tensor", "dp")),
        P(None, "tensor", "dp"),
        P(None, "dp", "tensor"),
        P(None, ("tensor", "dp")),
        P(None, "tensor", "dp"),
    )
    return jax.shard_map(
        per_device, mesh=mesh, in_specs=in_specs, out_specs=out_specs, check_vma=False
    )
```

profile of v0, /device:TPU:1, one launch (start us, length us, event | category | flops | bytes accessed | tf_op | source)
XLA Modules:
  0.0 1653.7 jit_solution(8090048458242188945)
XLA Ops:
  12.7 64.7 %all-gather.13 = f32[32,32,2]{1,2,0:T(2,128)S(1)} all-gather(f32[1,32,2]{1,2,0:T(2,128)S(1)} %bitcast.470), channel_id=1, replica_groups=mesh['dp'=8,'tensor'=4] {'dp','tensor'}, dimensions={0}, use_global_device_ids=true | all-gather | bytes 8448 | tf_op jit(solution)/shard_map/all_gather | solution.py:166
  77.6 63.6 %all-gather.12 = f32[32,32,2]{1,2,0:T(2,128)S(1)} all-gather(f32[1,32,2]{1,2,0:T(2,128)S(1)} %bitcast.471), channel_id=1, replica_groups=mesh['dp'=8,'tensor'=4] {'dp','tensor'}, dimensions={0}, use_global_device_ids=true | all-gather | bytes 8448 | tf_op jit(solution)/shard_map/all_gather | solution.py:165
  141.6 65.8 %all-gather.15 = f32[32,32,2]{1,2,0:T(2,128)S(1)} all-gather(f32[1,32,2]{1,2,0:T(2,128)S(1)} %bitcast.472), channel_id=1, replica_groups=mesh['dp'=8,'tensor'=4] {'dp','tensor'}, dimensions={0}, use_global_device_ids=true | all-gather | bytes 8448 | tf_op jit(solution)/shard_map/all_gather | solution.py:168
  208.1 63.5 %all-gather.14 = f32[32,32,2]{1,2,0:T(2,128)S(1)} all-gather(f32[1,32,2]{1,2,0:T(2,128)S(1)} %bitcast.473), channel_id=1, replica_groups=mesh['dp'=8,'tensor'=4] {'dp','tensor'}, dimensions={0}, use_global_device_ids=true | all-gather | bytes 8448 | tf_op jit(solution)/shard_map/all_gather | solution.py:167
  285.3 16.0 all-gather.1
  341.1 61.4 %all-gather.16 = f32[32,32,2]{1,2,0:T(2,128)S(1)} all-gather(f32[1,32,2]{1,2,0:T(2,128)S(1)} %bitcast.474), channel_id=1, replica_groups=mesh['dp'=8,'tensor'=4] {'dp','tensor'}, dimensions={0}, use_global_device_ids=true | all-gather | bytes 8448 | tf_op jit(solution)/shard_map/all_gather | solution.py:169
  415.6 16.4 all-gather.8
  479.1 16.8 %reduce-scatter.46.cloned.1.call-done = bf16[32,2,1024]{2,0,1:T(8,128)(2,1)} async-done(((bf16[128,2,1024]{2,0,1:T(8,128)(2,1)}), bf16[32,2,1024]{2,0,1:T(8,128)(2,1)}) %reduce-scatter.46.cloned.1.call-update) | async-done | bytes 131088 | tf_op jit(solution)/shard_map/reduce_scatter | solution.py:285
  497.8 18.6 %reduce-scatter.44.cloned.1.call-done = bf16[32,1024]{1,0:T(8,128)(2,1)} async-done(((bf16[128,1024]{1,0:T(8,128)(2,1)}), bf16[32,1024]{1,0:T(8,128)(2,1)}) %reduce-scatter.44.cloned.1.call-update) | async-done | bytes 65552 | tf_op jit(solution)/shard_map/reduce_scatter | solution.py:213
  545.7 17.2 %reduce-scatter.48.cloned.1.call-done = bf16[32,2,1024]{2,0,1:T(8,128)(2,1)} async-done(((bf16[128,2,1024]{2,0,1:T(8,128)(2,1)}), bf16[32,2,1024]{2,0,1:T(8,128)(2,1)}) %reduce-scatter.48.cloned.1.call-update) | async-done | bytes 131088 | tf_op jit(solution)/shard_map/reduce_scatter | solution.py:285
  599.7 36.3 %reduce-scatter.74.cloned.1.call-done = bf16[128,256]{1,0:T(8,128)(2,1)} async-done(((bf16[1024,256]{1,0:T(8,128)(2,1)}), bf16[128,256]{1,0:T(8,128)(2,1)}) %reduce-scatter.74.cloned.1.call-update) | async-done | bytes 65552
  650.1 22.5 %reduce-scatter.68.cloned.1.call-done = bf16[32,3]{1,0:T(8,128)(2,1)} async-done(((bf16[256,3]{1,0:T(8,128)(2,1)}), bf16[32,3]{1,0:T(8,128)(2,1)}) %reduce-scatter.68.cloned.1.call-update) | async-done | bytes 208
  673.9 132.9 %reduce-scatter.66.cloned.1.call-done = f32[32,2]{1,0:T(8,128)} async-done(((f32[1024,2]{1,0:T(8,128)}), f32[32,2]{1,0:T(8,128)}) %reduce-scatter.66.cloned.1.call-update) | async-done | bytes 272
  808.2 35.9 %reduce-scatter.72.cloned.1.call-done = bf16[128,256]{1,0:T(8,128)(2,1)} async-done(((bf16[1024,256]{1,0:T(8,128)(2,1)}), bf16[128,256]{1,0:T(8,128)(2,1)}) %reduce-scatter.72.cloned.1.call-update) | async-done | bytes 65552
  846.8 132.1 %reduce-scatter.58.cloned.1.call-done = f32[32,2]{1,0:T(8,128)} async-done(((f32[1024,2]{1,0:T(8,128)}), f32[32,2]{1,0:T(8,128)}) %reduce-scatter.58.cloned.1.call-update) | async-done | bytes 272
  980.2 133.6 %reduce-scatter.60.cloned.1.call-done = f32[32,2]{1,0:T(8,128)} async-done(((f32[1024,2]{1,0:T(8,128)}), f32[32,2]{1,0:T(8,128)}) %reduce-scatter.60.cloned.1.call-update) | async-done | bytes 272
  1115.2 133.1 %reduce-scatter.62.cloned.1.call-done = f32[32,2]{1,0:T(8,128)} async-done(((f32[1024,2]{1,0:T(8,128)}), f32[32,2]{1,0:T(8,128)}) %reduce-scatter.62.cloned.1.call-update) | async-done | bytes 272
  1249.6 133.1 %reduce-scatter.64.cloned.1.call-done = f32[32,2]{1,0:T(8,128)} async-done(((f32[1024,2]{1,0:T(8,128)}), f32[32,2]{1,0:T(8,128)}) %reduce-scatter.64.cloned.1.call-update) | async-done | bytes 272
  1384.1 43.5 %reduce-scatter.78.cloned.1.call-done = bf16[128,1024]{1,0:T(8,128)(2,1)} async-done(((bf16[1024,1024]{1,0:T(8,128)(2,1)}), bf16[128,1024]{1,0:T(8,128)(2,1)}) %reduce-scatter.78.cloned.1.call-update) | async-done | bytes 262160
  1428.7 40.5 %reduce-scatter.52.cloned.1.call-done = bf16[128,3,256]{2,0,1:T(8,128)(2,1)} async-done(((bf16[1024,3,256]{2,0,1:T(8,128)(2,1)}), bf16[128,3,256]{2,0,1:T(8,128)(2,1)}) %reduce-scatter.52.cloned.1.call-update) | async-done | bytes 196624 | tf_op jit(solution)/shard_map/reduce_scatter | solution.py:307
  1469.2 41.7 %reduce-scatter.50.cloned.1.call-done = bf16[128,3,256]{2,0,1:T(8,128)(2,1)} async-done(((bf16[1024,3,256]{2,0,1:T(8,128)(2,1)}), bf16[128,3,256]{2,0,1:T(8,128)(2,1)}) %reduce-scatter.50.cloned.1.call-update) | async-done | bytes 196624 | tf_op jit(solution)/shard_map/reduce_scatter | solution.py:307
  1512.8 42.5 %reduce-scatter.76.cloned.1.call-done = bf16[128,1024]{1,0:T(8,128)(2,1)} async-done(((bf16[1024,1024]{1,0:T(8,128)(2,1)}), bf16[128,1024]{1,0:T(8,128)(2,1)}) %reduce-scatter.76.cloned.1.call-update) | async-done | bytes 262160
  1556.5 43.1 %reduce-scatter.56.cloned.1.call-done = bf16[128,1024]{1,0:T(8,128)(2,1)} async-done(((bf16[1024,1024]{1,0:T(8,128)(2,1)}), bf16[128,1024]{1,0:T(8,128)(2,1)}) %reduce-scatter.56.cloned.1.call-update) | async-done | bytes 262160 | tf_op jit(solution)/shard_map/reduce_scatter | solution.py:316
  1599.6 44.4 %reduce-scatter.54.cloned.1.call-done = bf16[128,1024]{1,0:T(8,128)(2,1)} async-done(((bf16[1024,1024]{1,0:T(8,128)(2,1)}), bf16[128,1024]{1,0:T(8,128)(2,1)}) %reduce-scatter.54.cloned.1.call-update) | async-done | bytes 262160 | tf_op jit(solution)/shard_map/reduce_scatter | solution.py:316
  (446 shorter events, 217.9 us)
Async XLA Ops:
  7.3 313.1 %all-gather.24.cloned.1.call-start = ((), (), s32[]{:S(2)}) async-start(), calls=%async_computation.27 | async-start | bytes 1769472 | tf_op jit(solution)/shard_map/all_gather | solution.py:178
  9.2 315.9 %all-gather.26.cloned.1.call-start = ((), (), s32[]{:S(2)}) async-start(), calls=%async_computation.28 | async-start | bytes 2359296 | tf_op jit(solution)/shard_map/all_gather | solution.py:183
  11.2 316.2 %all-gather.28.cloned.1.call-start = ((), (), s32[]{:S(2)}) async-start(), calls=%async_computation.29 | async-start | bytes 2359296 | tf_op jit(solution)/shard_map/all_gather | solution.py:187
  12.1 431.0 %all-gather.30.cloned.1.call-start = ((), (), s32[]{:S(2)}) async-start(), calls=%async_computation.30 | async-start | bytes 1769472 | tf_op jit(solution)/shard_map/all_gather | solution.py:178
  12.6 432.2 %reduce-scatter.42.cloned.1.call-start = ((), (), s32[]{:S(2)}) async-start(), calls=%async_computation.19 | async-start | bytes 327680 | tf_op jit(solution)/shard_map/reduce_scatter | solution.py:213
  330.3 136.1 %all-gather.32.cloned.1.call-start = ((), (), s32[]{:S(2)}) async-start(), calls=%async_computation.31 | async-start | bytes 2359296 | tf_op jit(solution)/shard_map/all_gather | solution.py:183
  330.9 138.3 %all-gather.34.cloned.1.call-start = ((), (), s32[]{:S(2)}) async-start(), calls=%async_computation.32 | async-start | bytes 2359296 | tf_op jit(solution)/shard_map/all_gather | solution.py:187
  331.7 164.3 %reduce-scatter.46.cloned.1.call-start = ((), (), s32[]{:S(2)}) async-start(), calls=%async_computation.21 | async-start | bytes 655360 | tf_op jit(solution)/shard_map/reduce_scatter | solution.py:285
  479.1 83.9 %reduce-scatter.48.cloned.1.call-start = ((), (), s32[]{:S(2)}) async-start(), calls=%async_computation.22 | async-start | bytes 655360 | tf_op jit(solution)/shard_map/reduce_scatter | solution.py:285
  539.9 59.0 %reduce-scatter.70.cloned.1.call-start = ((), (), s32[]{:S(2)}) async-start(), calls=%async_computation.39 | async-start | bytes 73728
  540.8 95.2 %reduce-scatter.74.cloned.1.call-start = ((), (), s32[]{:S(2)}) async-start(), calls=%async_computation.41 | async-start | bytes 589824
  542.2 130.3 %reduce-scatter.68.cloned.1.call-start = ((), (), s32[]{:S(2)}) async-start(), calls=%async_computation.38 | async-start | bytes 73728
  543.1 263.7 %reduce-scatter.66.cloned.1.call-start = ((), (), s32[]{:S(2)}) async-start(), calls=%async_computation.37 | async-start | bytes 540672
  544.3 299.8 %reduce-scatter.72.cloned.1.call-start = ((), (), s32[]{:S(2)}) async-start(), calls=%async_computation.40 | async-start | bytes 589824
  545.7 433.2 %reduce-scatter.58.cloned.1.call-start = ((), (), s32[]{:S(2)}) async-start(), calls=%async_computation.33 | async-start | bytes 540672
  565.7 548.1 %reduce-scatter.60.cloned.1.call-start = ((), (), s32[]{:S(2)}) async-start(), calls=%async_computation.34 | async-start | bytes 540672
  566.9 681.4 %reduce-scatter.62.cloned.1.call-start = ((), (), s32[]{:S(2)}) async-start(), calls=%async_computation.35 | async-start | bytes 540672
  568.0 814.7 %reduce-scatter.64.cloned.1.call-start = ((), (), s32[]{:S(2)}) async-start(), calls=%async_computation.36 | async-start | bytes 540672
  569.1 858.5 %reduce-scatter.78.cloned.1.call-start = ((), (), s32[]{:S(2)}) async-start(), calls=%async_computation.43 | async-start | bytes 2359296
  573.7 895.5 %reduce-scatter.52.cloned.1.call-start = ((), (), s32[]{:S(2)}) async-start(), calls=%async_computation.24 | async-start | bytes 1769472 | tf_op jit(solution)/shard_map/reduce_scatter | solution.py:307
  576.5 934.4 %reduce-scatter.50.cloned.1.call-start = ((), (), s32[]{:S(2)}) async-start(), calls=%async_computation.23 | async-start | bytes 1769472 | tf_op jit(solution)/shard_map/reduce_scatter | solution.py:307
  578.5 976.8 %reduce-scatter.76.cloned.1.call-start = ((), (), s32[]{:S(2)}) async-start(), calls=%async_computation.42 | async-start | bytes 2359296
  583.0 1016.6 %reduce-scatter.56.cloned.1.call-start = ((), (), s32[]{:S(2)}) async-start(), calls=%async_computation.26 | async-start | bytes 2359296 | tf_op jit(solution)/shard_map/reduce_scatter | solution.py:316
  586.1 1057.9 %reduce-scatter.54.cloned.1.call-start = ((), (), s32[]{:S(2)}) async-start(), calls=%async_computation.25 | async-start | bytes 2359296 | tf_op jit(solution)/shard_map/reduce_scatter | solution.py:316
  (99 other events, 4382.8 us)
Sparse Core Ops, SparseCore 0:
  10.0 28.0 all-gather.23
  40.5 27.7 all-gather.25
  70.8 28.1 all-gather.27
  100.7 25.5 all-gather.29
  348.4 28.8 all-gather.31
  379.8 28.1 all-gather.33
  475.7 20.2 reduce-scatter.45
  498.8 17.5 reduce-scatter.43
  540.0 22.9 reduce-scatter.47
  566.0 32.8 reduce-scatter.69
  601.8 34.1 reduce-scatter.73
  639.0 33.5 reduce-scatter.67
  674.6 132.1 reduce-scatter.65
  809.7 34.2 reduce-scatter.71
  846.7 132.1 reduce-scatter.57
  981.6 132.2 reduce-scatter.59
  1115.9 132.2 reduce-scatter.61
  1250.5 132.2 reduce-scatter.63
  1385.9 41.6 reduce-scatter.77
  1430.9 38.2 reduce-scatter.51
  1472.5 38.3 reduce-scatter.49
  1514.2 41.1 reduce-scatter.75
  1558.5 41.0 reduce-scatter.55
  1602.9 41.0 reduce-scatter.53
  (1 shorter events, 15.6 us)
where the time goes:
time: 1660 us; the launch traced here: 1650 us
  waiting for transfers between devices  1080 us (65%)
  blocking collectives  449 us (27%)
  local copies, waits for them, and re-layouts  47 us (3%)
  matrix products  39.9 us (2%)
  other arithmetic  20.2 us (1%)
    unnamed x36, waiting for transfers between devices  857 us
    reduce_scatter x2, waiting for transfers between devices, per_device(): lax.psum_scatter(grad_fc_mat.astype(jnp.bfloat16), 'dp', scatter_dimensio...  87.6 us
    reduce_scatter x2, waiting for transfers between devices, per_device(): lax.psum_scatter(grad_qkv_mat.astype(jnp.bfloat16), 'dp', scatter_dimensi...  82.2 us
    all_gather x1, blocking collectives, per_device(): lax.all_gather(ln2_bias, ('dp', 'tensor'), axis=1, tiled=True)  65.8 us
    all_gather x1, blocking collectives, per_device(): lax.all_gather(ln1_bias, ('dp', 'tensor'), axis=1, tiled=True)  64.7 us
    all_gather x1, blocking collectives, per_device(): lax.all_gather(ln1_gain, ('dp', 'tensor'), axis=1, tiled=True)  63.6 us
    all_gather x1, blocking collectives, per_device(): lax.all_gather(ln2_gain, ('dp', 'tensor'), axis=1, tiled=True)  63.5 us
    all_gather x1, blocking collectives, per_device(): lax.all_gather(res_bias, ('dp', 'tensor'), axis=1, tiled=True)  61.4 us
  transfers between devices with their start and end apart: 25, of which 18 were waited for; matrix products, arithmetic and copies ran while one was open for 5% of the time, Pallas kernels for 0%

commit v1 on v0

v1 whole, which is shorter than its diff:
```python
import functools

import jax
import jax.numpy as jnp
from jax import lax
from jax.experimental import pallas as pl
from jax.experimental.pallas import tpu as pltpu
from jax.sharding import PartitionSpec as P

HD = 64
ROT = 16


EPS = 1e-05
NEG_FILL = -1e30


def gelu_exact(values):
    return 0.5 * values * (1.0 + jax.scipy.special.erf(values * 0.7071067811865476))


def gelu_slope(values):
    normal_cdf = 0.5 * (1.0 + jax.scipy.special.erf(values * 0.7071067811865476))
    return normal_cdf + values * jnp.exp(-0.5 * values * values) * 0.3989422804014327


def group_layout(seq_len, total_rows):
    ends = jnp.cumsum(seq_len)
    starts = ends - seq_len
    row_ids = jnp.arange(total_rows, dtype=jnp.int32)
    member = (row_ids[:, None] >= starts[None, :]) & (row_ids[:, None] < ends[None, :])
    seq_index = jnp.arange(seq_len.shape[0], dtype=jnp.int32)
    seq_ids = jnp.sum(jnp.where(member, seq_index[None, :], 0), axis=1)
    row_start = jnp.sum(jnp.where(member, starts[None, :], 0), axis=1)
    return (seq_ids, row_ids - row_start, row_ids)


def rotary_tables(positions):
    half_rot = ROT // 2
    freq_ids = jnp.arange(half_rot, dtype=jnp.float32)
    inverse = jnp.power(10000.0, -2.0 * freq_ids / ROT)
    angles = positions.astype(jnp.float32)[:, None] * inverse[None, :]
    return (jnp.cos(angles), jnp.sin(angles))


def rotate(vectors, cos_tab, sin_tab, direction_sign):
    half_rot = ROT // 2
    lower_half = vectors[..., :half_rot]
    upper_half = vectors[..., half_rot:ROT]
    cos_b = cos_tab[:, None, :]
    sin_b = sin_tab[:, None, :]
    new_lower = lower_half * cos_b - direction_sign * upper_half * sin_b
    new_upper = upper_half * cos_b + direction_sign * lower_half * sin_b
    return jnp.concatenate([new_lower, new_upper, vectors[..., ROT:]], axis=-1)


def masked_block(q_blk, keys, q_seq, q_row, seq_ids, row_ids):
    scores = jnp.einsum("qhd,khd->hqk", q_blk, keys, preferred_element_type=jnp.float32) * HD ** (
        -0.5
    )
    allowed = (q_seq[:, None] == seq_ids[None, :]) & (row_ids[None, :] <= q_row[:, None])
    return jnp.where(allowed[None], scores, NEG_FILL)


def attention_forward(queries, keys, values, seq_ids, row_ids):
    total_rows, heads_here, head_dim = queries.shape
    block_rows = min(512, total_rows)
    blocks = total_rows // block_rows

    def one_block(inputs):
        q_blk, q_seq, q_row = inputs
        scores = masked_block(q_blk, keys, q_seq, q_row, seq_ids, row_ids)
        top_val = jnp.max(scores, axis=-1, keepdims=True)
        exponent_terms = jnp.exp(scores - top_val)
        totals = jnp.sum(exponent_terms, axis=-1, keepdims=True)
        attn_probs = (exponent_terms / totals).astype(jnp.bfloat16)
        context = jnp.einsum(
            "hqk,khd->qhd", attn_probs, values, preferred_element_type=jnp.float32
        ).astype(jnp.bfloat16)
        return (context, (top_val + jnp.log(totals))[..., 0])

    contexts, log_totals = lax.map(
        one_block,
        (
            queries.reshape(blocks, block_rows, heads_here, head_dim),
            seq_ids.reshape(blocks, block_rows),
            row_ids.reshape(blocks, block_rows),
        ),
    )
    return (contexts.reshape(total_rows, heads_here, head_dim), log_totals)


def attention_backward(queries, keys, values, contexts, d_context, log_totals, seq_ids, row_ids):
    total_rows, heads_here, head_dim = queries.shape
    block_rows = min(512, total_rows)
    blocks = total_rows // block_rows

    def one_block(carry, inputs):
        d_keys, d_values = carry
        q_blk, c_blk, dc_blk, lse_blk, q_seq, q_row = inputs
        scores = masked_block(q_blk, keys, q_seq, q_row, seq_ids, row_ids)
        probs_full = jnp.exp(scores - lse_blk[..., None])
        d_probs = jnp.einsum("qhd,khd->hqk", dc_blk, values, preferred_element_type=jnp.float32)
        delta = jnp.sum(dc_blk.astype(jnp.float32) * c_blk.astype(jnp.float32), axis=-1)
        d_scores = probs_full * (d_probs - jnp.transpose(delta)[:, :, None])
        d_scaled = (d_scores * HD ** (-0.5)).astype(jnp.bfloat16)
        d_q = jnp.einsum("hqk,khd->qhd", d_scaled, keys, preferred_element_type=jnp.float32)
        d_keys = d_keys + jnp.einsum(
            "hqk,qhd->khd", d_scaled, q_blk, preferred_element_type=jnp.float32
        )
        d_values = d_values + jnp.einsum(
            "hqk,qhd->khd",
            probs_full.astype(jnp.bfloat16),
            dc_blk,
            preferred_element_type=jnp.float32,
        )
        return ((d_keys, d_values), d_q)

    zero_keys = jnp.zeros(keys.shape, jnp.float32)
    shape_blk = (blocks, block_rows, heads_here, head_dim)
    carry_out, d_queries = lax.scan(
        one_block,
        (zero_keys, zero_keys),
        (
            queries.reshape(shape_blk),
            contexts.reshape(shape_blk),
            d_context.reshape(shape_blk),
            log_totals,
            seq_ids.reshape(blocks, block_rows),
            row_ids.reshape(blocks, block_rows),
        ),
    )
    return (d_queries.reshape(total_rows, heads_here, head_dim), carry_out[0], carry_out[1])


MESH = pl.DeviceIdType.MESH
ANY = pl.BlockSpec(memory_space=pl.ANY)
VMEM = pl.BlockSpec(memory_space=pltpu.VMEM)
N_SEMS = 160
N_LOCAL = 32


class Links:
    def __init__(self, n_dp, n_tensor, send_sems, recv_sems, local_sems):
        self.n_dp, self.n_tensor = n_dp, n_tensor
        self.dp, self.tensor = lax.axis_index("dp"), lax.axis_index("tensor")
        self.send_sems, self.recv_sems, self.local_sems = send_sems, recv_sems, local_sems
        self.used, self.used_local = 0, 0
        self.sent = []

    def send(self, src, dst, **where):
        copy = pltpu.make_async_remote_copy(
            src_ref=src,
            dst_ref=dst,
            send_sem=self.send_sems.at[self.used],
            recv_sem=self.recv_sems.at[self.used],
            device_id=where,
            device_id_type=MESH,
        )
        self.used += 1
        copy.start()
        self.sent.append(copy)
        return copy

    def local(self, src, dst):
        copy = pltpu.make_async_copy(src, dst, self.local_sems.at[self.used_local])
        self.used_local += 1
        copy.start()
        return copy

    def dp_peer(self, step):
        return lax.rem(self.dp + step, self.n_dp)

    def tensor_peer(self, step):
        return lax.rem(self.tensor + step, self.n_tensor)

    def tensor_from(self, step):
        return lax.rem(self.tensor + self.n_tensor - step, self.n_tensor)

    def barrier(self, with_dp):
        sem = pltpu.get_barrier_semaphore()
        count = self.n_tensor - 1
        for step in range(1, self.n_tensor):
            pl.semaphore_signal(
                sem, inc=1, device_id={"tensor": self.tensor_peer(step)}, device_id_type=MESH
            )
        if with_dp:
            count += self.n_dp - 1
            for step in range(1, self.n_dp):
                pl.semaphore_signal(
                    sem, inc=1, device_id={"dp": self.dp_peer(step)}, device_id_type=MESH
                )
        pl.semaphore_wait(sem, count)

    def finish(self):
        for copy in self.sent:
            copy.wait_send()


def start_dp_gather(links, items):
    chips = links.n_dp // 2
    core, chip = lax.rem(links.dp, 2), links.dp // 2
    partner = links.dp + 1 - 2 * core
    direct = []
    for step in range(1, chips):
        peer = lax.rem(chip + step, chips) * 2 + core
        for own, slot in items:
            direct.append(links.send(own, slot(links.dp), dp=peer))
    passed = [links.send(own, slot(links.dp), dp=partner) for own, slot in items]
    return direct, passed


def end_dp_gather(links, items, direct, passed):
    chips = links.n_dp // 2
    core, chip = lax.rem(links.dp, 2), links.dp // 2
    partner = links.dp + 1 - 2 * core
    position = 0
    for step in range(1, chips):
        origin = lax.rem(chip + chips - step, chips) * 2 + core
        for _, slot in items:
            direct[position].wait_recv()
            position += 1
            passed.append(links.send(slot(origin), slot(origin), dp=partner))
    for copy in passed:
        copy.wait_recv()


def row_slot(ref, rows):
    return lambda d: ref.at[pl.ds(pl.multiple_of(d * rows, rows), rows)]


def weight_slot(ref, layer, axis, size):
    if axis is None:
        return lambda d: ref.at[d, layer]
    if axis == 0:
        return lambda d: ref.at[layer, pl.ds(pl.multiple_of(d * size, size), size), :]
    return lambda d: ref.at[layer, :, pl.ds(pl.multiple_of(d * size, size), size)]


def scratch_sems():
    return [
        pltpu.SemaphoreType.DMA((N_SEMS,)),
        pltpu.SemaphoreType.DMA((N_SEMS,)),
        pltpu.SemaphoreType.DMA((N_LOCAL,)),
    ]


def entry_kernel(n_dp, n_tensor, axes, *refs):
    n_w = len(axes)
    w_in, (small_in, rows_in) = refs[:n_w], refs[n_w : n_w + 2]
    w_out = refs[n_w + 2 : 2 * n_w + 2]
    small_out, rows_out = refs[2 * n_w + 2 : 2 * n_w + 4]
    held = refs[2 * n_w + 4 : 3 * n_w + 4]
    links = Links(n_dp, n_tensor, *refs[3 * n_w + 4 :])
    loads = [links.local(src, dst) for src, dst in zip(w_in, held)]
    links.barrier(True)
    layers = w_in[0].shape[0]
    small_own = links.local(small_in, small_out.at[links.tensor, links.dp])
    row_count = rows_in.shape[0]
    slot = row_slot(rows_out, row_count)
    rows_own = links.local(rows_in, slot(links.tensor))
    rows_sent = [
        links.send(rows_in, slot(links.tensor), tensor=links.tensor_peer(step))
        for step in range(1, n_tensor)
    ]
    small_sent = [
        links.send(small_in, small_out.at[links.tensor, links.dp], dp=links.dp_peer(step))
        for step in range(1, n_dp)
    ]
    for copy in loads:
        copy.wait()
    items = []
    for layer in range(layers):
        for index, axis in enumerate(axes):
            size = w_in[index].shape[1 + axis] if axis is not None else 0
            items.append(
                (held[index].at[layer], weight_slot(w_out[index], layer, axis, size))
            )
    direct, passed = start_dp_gather(links, items)
    own = [links.local(src, slot_of(links.dp)) for src, slot_of in items]
    small_own.wait()
    for copy in small_sent:
        copy.wait_recv()
    small_wide = [
        links.send(
            small_out.at[links.tensor], small_out.at[links.tensor], tensor=links.tensor_peer(step)
        )
        for step in range(1, n_tensor)
    ]
    end_dp_gather(links, items, direct, passed)
    for copy in rows_sent + small_wide:
        copy.wait_recv()
    rows_own.wait()
    for copy in own:
        copy.wait()
    links.finish()


def start_scatter(links, part, landing):
    rows = landing.shape[1]
    return [
        links.send(
            row_slot(part, rows)(links.tensor_peer(step)),
            landing.at[step - 1],
            tensor=links.tensor_peer(step),
        )
        for step in range(1, links.n_tensor)
    ]


def end_scatter(links, part, landing, copies):
    rows = landing.shape[1]
    total = part[pl.ds(pl.multiple_of(links.tensor * rows, rows), rows), :].astype(jnp.float32)
    for step, copy in enumerate(copies):
        copy.wait_recv()
        total = total + landing[step].astype(jnp.float32)
    return total


def start_gather(links, out, own):
    rows = own.shape[0]
    slot = row_slot(out, rows)
    copies = [
        links.send(own, slot(links.tensor), tensor=links.tensor_peer(step))
        for step in range(1, links.n_tensor)
    ]
    return copies, links.local(own, slot(links.tensor))


def unit_rows(values):
    average = jnp.mean(values, axis=-1, keepdims=True)
    centred = values - average
    variance = jnp.mean(centred * centred, axis=-1, keepdims=True)
    scale = lax.rsqrt(variance + EPS)
    return centred * scale, scale


def back_unit(values, grad):
    unit, scale = unit_rows(values)
    return scale * (
        grad
        - jnp.mean(grad, axis=-1, keepdims=True)
        - unit * jnp.mean(grad * unit, axis=-1, keepdims=True)
    )


def forward_kernel(n_dp, n_tensor, part, resid, bias, new_resid, rows_out, landing, own, *sems):
    links = Links(n_dp, n_tensor, *sems)
    links.barrier(False)
    branch = end_scatter(links, part, landing, start_scatter(links, part, landing))
    values = resid[...] + branch + bias[...]
    new_resid[...] = values
    own[...] = unit_rows(values)[0].astype(jnp.bfloat16)
    copies, local = start_gather(links, rows_out, own)
    for copy in copies:
        copy.wait_recv()
    local.wait()
    links.finish()


def backward_kernel(
    n_dp, n_tensor, part_y, part_e, resid, bias, dres, y_out, d_out, rows_out, land_y, land_e, own, *sems
):
    links = Links(n_dp, n_tensor, *sems)
    links.barrier(False)
    copies_e = start_scatter(links, part_e, land_e)
    copies_y = start_scatter(links, part_y, land_y) if part_y is not None else None
    grad = end_scatter(links, part_e, land_e, copies_e)
    values = resid[...]
    new_d = dres[...] + back_unit(values, grad)
    d_out[...] = new_d
    own[...] = new_d.astype(jnp.bfloat16)
    copies, local = start_gather(links, rows_out, own)
    if part_y is not None:
        y_out[...] = values + end_scatter(links, part_y, land_y, copies_y) + bias[...]
    for copy in copies:
        copy.wait_recv()
    local.wait()
    links.finish()


def exit_kernel(n_dp, n_tensor, n_act, *refs):
    acts, refs = refs[:n_act], refs[n_act:]
    cross, small, part_e, resid, dres = refs[:5]
    act_out, refs = refs[5 : 5 + n_act], refs[5 + n_act :]
    cross_out, small_out, d_out = refs[:3]
    held, refs = refs[3 : 3 + n_act], refs[3 + n_act :]
    land_e, land_s, half_s, land_t = refs[:4]
    links = Links(n_dp, n_tensor, *refs[4:])
    loads = [links.local(src, dst) for src, dst in zip(acts, held)]
    links.barrier(True)
    copies_e = start_scatter(links, part_e, land_e)
    small_sent = [
        links.send(small.at[links.dp_peer(step)], land_s.at[step - 1], dp=links.dp_peer(step))
        for step in range(1, n_dp)
    ]
    for copy in loads:
        copy.wait()
    items = [
        (own, row_slot(ref, own.shape[0])) for own, ref in zip(held, act_out)
    ]
    direct, passed = start_dp_gather(links, items)
    cross_sent = [
        links.send(cross.at[links.dp_peer(step)], cross_out.at[links.dp], dp=links.dp_peer(step))
        for step in range(1, n_dp)
    ]
    own = [links.local(src, slot_of(links.dp)) for src, slot_of in items]
    own.append(links.local(cross.at[links.dp], cross_out.at[links.dp]))
    total = small[links.dp]
    for step, copy in enumerate(small_sent):
        copy.wait_recv()
        total = total + land_s[step]
    half_s[...] = total
    wide = [
        links.send(half_s, land_t.at[step - 1], tensor=links.tensor_peer(step))
        for step in range(1, n_tensor)
    ]
    grad = end_scatter(links, part_e, land_e, copies_e)
    d_out[...] = dres[...] + back_unit(resid[...], grad)
    for step, copy in enumerate(wide):
        copy.wait_recv()
        total = total + land_t[step]
    small_out[...] = total
    end_dp_gather(links, items, direct, passed)
    for copy in cross_sent:
        copy.wait_recv()
    for copy in own:
        copy.wait()
    links.finish()


def call(kernel, name, collective, outs, out_specs, in_specs, scratch, args):
    return pl.pallas_call(
        kernel,
        out_shape=outs,
        in_specs=in_specs,
        out_specs=out_specs,
        scratch_shapes=scratch + scratch_sems(),
        name=name,
        compiler_params=pltpu.CompilerParams(
            collective_id=collective, has_side_effects=True, vmem_limit_bytes=40 << 20
        ),
    )(*args)


def shaped(shape, dtype):
    return jax.ShapeDtypeStruct(tuple(shape), dtype)


def pack_rows(parts):
    flat = jnp.concatenate([part.reshape(-1) for part in parts])
    padded = -(-flat.shape[0] // 1024) * 1024
    return jnp.pad(flat, (0, padded - flat.shape[0])).reshape(-1, 128)


def per_device(
    x_in,
    seq_lengths,
    ln1_gain,
    ln1_bias,
    ln2_gain,
    ln2_bias,
    res_bias,
    w_qkv,
    b_qkv,
    w_out,
    w_fc,
    b_fc,
    w_proj,
    grad_out,
):
    n_tensor, n_dp = lax.axis_size("tensor"), lax.axis_size("dp")
    my_tensor = lax.axis_index("tensor")
    bf16, f32 = jnp.bfloat16, jnp.float32
    my_rows, width = x_in.shape
    group_rows = my_rows * n_tensor
    total_rows = group_rows * n_dp
    layer_count = w_qkv.shape[0]
    heads_here = w_qkv.shape[3] // HD
    dp_width = width // n_dp
    vec_width = dp_width // n_tensor

    columns_ok = dp_width % 128 == 0
    shards = (w_qkv.reshape(layer_count, dp_width, -1), w_out, w_fc, w_proj)
    axes = (0, 1 if columns_ok else None, 0, 1 if columns_ok else None)
    gathered = []
    for shard, axis in zip(shards, axes):
        shape = list(shard.shape)
        if axis is None:
            shape = [n_dp] + shape
        else:
            shape[1 + axis] *= n_dp
        gathered.append(shaped(shape, bf16))
    smalls = (
        jnp.stack([ln1_gain, ln1_bias, ln2_gain, ln2_bias, res_bias]),
        b_qkv,
        b_fc,
    )
    packed = pack_rows(smalls)
    unit_first = unit_rows(x_in)[0].astype(bf16)
    rows_first = jnp.concatenate([unit_first, grad_out.astype(bf16)], axis=1)
    entry = call(
        functools.partial(entry_kernel, n_dp, n_tensor, axes),
        "entry",
        0,
        tuple(gathered)
        + (
            shaped((n_tensor, n_dp) + packed.shape, f32),
            shaped((group_rows, 2 * width), bf16),
        ),
        (ANY,) * 4 + (VMEM, VMEM),
        [ANY] * 4 + [VMEM, VMEM],
        [pltpu.VMEM(shard.shape, bf16) for shard in shards],
        shards + (packed, rows_first),
    )
    qkv_all, out_all, fc_all, proj_all, small_all, rows_all = entry
    if not columns_ok:
        out_all = jnp.transpose(out_all, (1, 2, 0, 3)).reshape(layer_count, -1, width)
        proj_all = jnp.transpose(proj_all, (1, 2, 0, 3)).reshape(layer_count, -1, width)
    small_all = small_all.reshape(n_tensor, n_dp, -1)
    n_gain = smalls[0].size
    vectors = jnp.transpose(
        small_all[:, :, :n_gain].reshape(n_tensor, n_dp, 5, layer_count, vec_width),
        (2, 3, 1, 0, 4),
    ).reshape(5, layer_count, width)
    gain_one, bias_one, gain_two, bias_two, out_bias = vectors
    mine = lax.dynamic_index_in_dim(small_all, my_tensor, 0, keepdims=False)
    qkv_vecs = jnp.transpose(
        mine[:, n_gain : n_gain + b_qkv.size].reshape((n_dp,) + b_qkv.shape), (1, 2, 0, 3)
    ).reshape(layer_count, 1, -1)
    fc_vecs = jnp.transpose(
        mine[:, n_gain + b_qkv.size : n_gain + b_qkv.size + b_fc.size].reshape(
            (n_dp,) + b_fc.shape
        ),
        (1, 0, 2),
    ).reshape(layer_count, 1, -1)

    seq_ids, positions, row_ids = group_layout(seq_lengths[0], group_rows)
    cos_tab, sin_tab = rotary_tables(positions)
    unit_full, d_rows = rows_all[:, :width], rows_all[:, width:]
    resid = x_in
    saved = []
    for layer in range(layer_count):
        unit_wide = unit_full.astype(f32)
        normed_a = (unit_wide * gain_one[layer] + bias_one[layer]).astype(bf16)
        normed_m = (unit_wide * gain_two[layer] + bias_two[layer]).astype(bf16)
        projected = (
            jnp.dot(normed_a, qkv_all[layer], preferred_element_type=f32) + qkv_vecs[layer]
        )
        split_heads = projected.reshape(group_rows, 3, heads_here, HD)
        queries = rotate(split_heads[:, 0], cos_tab, sin_tab, 1.0).astype(bf16)
        keys = rotate(split_heads[:, 1], cos_tab, sin_tab, 1.0).astype(bf16)
        values = split_heads[:, 2].astype(bf16)
        contexts, log_totals = attention_forward(queries, keys, values, seq_ids, row_ids)
        hidden_pre = jnp.dot(normed_m, fc_all[layer], preferred_element_type=f32) + fc_vecs[layer]
        activated = gelu_exact(hidden_pre).astype(bf16)
        flat_context = contexts.reshape(group_rows, -1)
        partial = (
            jnp.dot(flat_context, out_all[layer], preferred_element_type=f32)
            + jnp.dot(activated, proj_all[layer], preferred_element_type=f32)
        ).astype(bf16)
        saved.append(
            (resid, unit_full, queries, keys, values, contexts, log_totals, hidden_pre, activated)
        )
        if layer + 1 < layer_count:
            resid, unit_full = call(
                functools.partial(forward_kernel, n_dp, n_tensor),
                f"forward{layer}",
                1 + layer,
                (shaped(x_in.shape, f32), shaped((group_rows, width), bf16)),
                (VMEM, VMEM),
                [VMEM] * 3,
                [
                    pltpu.VMEM((n_tensor - 1, my_rows, width), bf16),
                    pltpu.VMEM((my_rows, width), bf16),
                ],
                (partial, resid, out_bias[layer][None]),
            )
    d_resid = grad_out
    acts, cross, sums = [None] * layer_count, [None] * layer_count, [None] * layer_count
    y_out = None
    for layer in reversed(range(layer_count)):
        (
            layer_input,
            unit_full,
            queries,
            keys,
            values,
            contexts,
            log_totals,
            hidden_pre,
            activated,
        ) = saved[layer]
        out_bias_grad = jnp.sum(d_resid, axis=0)
        flat_context = contexts.reshape(group_rows, -1)
        transposed = (((1,), (1,)), ((), ()))
        d_context = lax.dot_general(
            d_rows, out_all[layer], transposed, preferred_element_type=f32
        ).astype(bf16)
        d_act = lax.dot_general(d_rows, proj_all[layer], transposed, preferred_element_type=f32)
        d_pre_b = (d_act * gelu_slope(hidden_pre)).astype(bf16)
        d_queries, d_keys, d_values = attention_backward(
            queries,
            keys,
            values,
            contexts,
            d_context.reshape(group_rows, heads_here, HD),
            log_totals,
            seq_ids,
            row_ids,
        )
        d_queries = rotate(d_queries, cos_tab, sin_tab, -1.0)
        d_keys = rotate(d_keys, cos_tab, sin_tab, -1.0)
        flat_dqkv = (
            jnp.stack([d_queries, d_keys, d_values], axis=1).reshape(group_rows, -1).astype(bf16)
        )
        d_a = lax.dot_general(flat_dqkv, qkv_all[layer], transposed, preferred_element_type=f32)
        d_m = lax.dot_general(d_pre_b, fc_all[layer], transposed, preferred_element_type=f32)
        unit_wide = unit_full.astype(f32)
        sums[layer] = (
            jnp.sum(d_a * unit_wide, axis=0),
            jnp.sum(d_a, axis=0),
            jnp.sum(d_m * unit_wide, axis=0),
            jnp.sum(d_m, axis=0),
            out_bias_grad,
        )
        part_e = (d_a * gain_one[layer] + d_m * gain_two[layer]).astype(bf16)
        acts[layer] = (flat_context, activated, flat_dqkv, d_pre_b)
        cross[layer] = jnp.stack([unit_full, d_rows]).reshape(2, group_rows, n_dp, dp_width)
        land = pltpu.VMEM((n_tensor - 1, my_rows, width), bf16)
        if layer > 0:
            last = layer + 1 == layer_count
            d_shape = shaped(x_in.shape, f32)
            rows_shape = shaped((group_rows, width), bf16)
            own = pltpu.VMEM((my_rows, width), bf16)
            if last:
                y_out, d_resid, d_rows = call(
                    functools.partial(backward_kernel, n_dp, n_tensor),
                    f"backward{layer}",
                    layer_count + layer,
                    (d_shape, d_shape, rows_shape),
                    (VMEM,) * 3,
                    [VMEM] * 5,
                    [land, land, own],
                    (partial, part_e, layer_input, out_bias[layer][None], d_resid),
                )
            else:

                def no_y(e, r, d, d_o, r_o, l_e, o, *sems):
                    backward_kernel(
                        n_dp, n_tensor, None, e, r, None, d, None, d_o, r_o, None, l_e, o, *sems
                    )

                d_resid, d_rows = call(
                    no_y,
                    f"backward{layer}",
                    layer_count + layer,
                    (d_shape, rows_shape),
                    (VMEM,) * 2,
                    [VMEM] * 3,
                    [land, own],
                    (part_e, layer_input, d_resid),
                )
    flat_acts = [array for group in acts for array in group]
    n_act = len(flat_acts)
    cross_in = jnp.transpose(jnp.stack(cross), (3, 0, 1, 2, 4))
    stacked = jnp.stack([jnp.stack(group) for group in sums]).reshape(-1, width)
    n_sums = stacked.shape[0]
    padded = -(-n_sums // 8) * 8
    small_in = jnp.transpose(
        jnp.pad(stacked, ((0, padded - n_sums), (0, 0))).reshape(padded, n_dp, dp_width), (1, 0, 2)
    )
    small_block = (padded, dp_width)
    results = call(
        functools.partial(exit_kernel, n_dp, n_tensor, n_act),
        "exit",
        2 * layer_count,
        tuple(shaped((total_rows, array.shape[1]), bf16) for array in flat_acts)
        + (shaped(cross_in.shape, bf16), shaped(small_block, f32), shaped(x_in.shape, f32)),
        (ANY,) * n_act + (VMEM,) * 3,
        [ANY] * n_act + [VMEM] * 5,
        [pltpu.VMEM(array.shape, bf16) for array in flat_acts]
        + [
            land,
            pltpu.VMEM((n_dp - 1,) + small_block, f32),
            pltpu.VMEM(small_block, f32),
            pltpu.VMEM((n_tensor - 1,) + small_block, f32),
        ],
        tuple(flat_acts) + (cross_in, small_in, part_e, layer_input, d_resid),
    )
    all_acts, (cross_all, small_sum, grad_x) = results[:n_act], results[n_act:]
    my_dp = lax.axis_index("dp")
    over_tokens = (((0,), (0,)), ((), ()))
    grads = [[] for _ in range(6)]
    for layer in range(layer_count):
        context_t, act_t, dqkv_t, d_pre_t = all_acts[4 * layer : 4 * layer + 4]
        unit_t = cross_all[:, layer, 0].reshape(total_rows, dp_width).astype(f32)
        d_t = cross_all[:, layer, 1].reshape(total_rows, dp_width)

        def here(vector):
            return lax.dynamic_slice_in_dim(vector[layer], my_dp * dp_width, dp_width)

        a_t = (unit_t * here(gain_one) + here(bias_one)).astype(bf16)
        m_t = (unit_t * here(gain_two) + here(bias_two)).astype(bf16)

        def contract(left, right):
            return lax.dot_general(left, right, over_tokens, preferred_element_type=f32)

        qkv_sums = jnp.sum(dqkv_t.astype(f32), axis=0).reshape(3, -1)
        fc_sums = jnp.sum(d_pre_t.astype(f32), axis=0)
        grads[0].append(contract(a_t, dqkv_t).reshape(w_qkv.shape[1:]))
        grads[1].append(
            lax.dynamic_slice_in_dim(qkv_sums, my_dp * b_qkv.shape[2], b_qkv.shape[2], axis=1)
        )
        grads[2].append(contract(context_t, d_t))
        grads[3].append(contract(m_t, d_pre_t))
        grads[4].append(lax.dynamic_slice_in_dim(fc_sums, my_dp * b_fc.shape[1], b_fc.shape[1]))
        grads[5].append(contract(act_t, d_t))
    stacked_grads = tuple(jnp.stack(group) for group in grads)
    vector_grads = lax.dynamic_slice_in_dim(
        small_sum[:n_sums].reshape(layer_count, 5, dp_width), my_tensor * vec_width, vec_width, axis=2
    )
    return (
        y_out,
        grad_x,
        vector_grads[:, 0],
        vector_grads[:, 1],
        vector_grads[:, 2],
        vector_grads[:, 3],
        vector_grads[:, 4],
    ) + stacked_grads


def solution(mesh):
    in_specs = (
        P(("dp", "tensor"), None),
        P("dp", None),
        P(None, ("dp", "tensor")),
        P(None, ("dp", "tensor")),
        P(None, ("dp", "tensor")),
        P(None, ("dp", "tensor")),
        P(None, ("dp", "tensor")),
        P(None, "dp", None, "tensor"),
        P(None, None, ("tensor", "dp")),
        P(None, "tensor", "dp"),
        P(None, "dp", "tensor"),
        P(None, ("tensor", "dp")),
        P(None, "tensor", "dp"),
        P(("dp", "tensor"), None),
    )
    out_specs = (
        P(("dp", "tensor"), None),
        P(("dp", "tensor"), None),
        P(None, ("dp", "tensor")),
        P(None, ("dp", "tensor")),
        P(None, ("dp", "tensor")),
        P(None, ("dp", "tensor")),
        P(None, ("dp", "tensor")),
        P(None, "dp", None, "tensor"),
        P(None, None, ("tensor", "dp")),
        P(None, "tensor", "dp"),
        P(None, "dp", "tensor"),
        P(None, ("tensor", "dp")),
        P(None, "tensor", "dp"),
    )
    return jax.shard_map(
        per_device, mesh=mesh, in_specs=in_specs, out_specs=out_specs, check_vma=False
    )
```

time: 1660 us -> 341 us (0.21)
  waiting for transfers between devices: 1080 us -> 0 us
  blocking collectives: 449 us -> 0 us
  Pallas kernels: 0 us -> 211 us
  local copies, waits for them, and re-layouts: 47 us -> 63.8 us
    unnamed x36 -> x0, waiting for transfers between devices: 857 us -> none
    all_gather x15 -> x0, blocking collectives: 437 us -> none  [the longest x1 65.8 us: per_device(): lax.all_gather(ln2_bias, ('dp', 'tensor'), axis=1, tiled=True)]
    reduce_scatter x8 -> x0, waiting for transfers between devices: 222 us -> none  [the longest x2 87.6 us: per_device(): lax.psum_scatter(grad_fc_mat.astype(jnp.bfloat16), 'dp', scatter_dimensio...]
    pallas_call x0 -> x4, Pallas kernels: none -> 211 us  [call(): pl.pallas_call(kernel, out_shape=outs, in_specs=in_specs, out_specs=out_s...]
    unnamed x228 -> x251, local copies, waits for them, and re-layouts: 34.1 us -> 30.7 us
  transfers between devices with their start and end apart: 25 -> 0, of which waited for: 18 -> 0; matrix products, arithmetic and copies ran while one was open for 5% -> 0% of each run, Pallas kernels for 0% -> 0%
where the time goes in v1:
time: 341 us; the launch traced here: 339 us
  Pallas kernels  211 us (62%)
  local copies, waits for them, and re-layouts  63.8 us (19%)
  matrix products  46.5 us (14%)
  other arithmetic  15.9 us (5%)
    pallas_call x4, Pallas kernels, call(): pl.pallas_call(kernel, out_shape=outs, in_specs=in_specs, out_specs=out_s...  211 us
    unnamed x251, local copies, waits for them, and re-layouts  30.7 us

profile of v1, /device:TPU:1, one launch (start us, length us, event | category | flops | bytes accessed | tf_op | source)
XLA Modules:
  0.0 339.1 jit_solution(6613033361040599908)
XLA Ops:
  2.9 1.7 fusion.158
  10.2 82.4 %entry.1 = (bf16[2,1024,768]{2,1,0:T(8,128)(2,1)S(1)}, bf16[2,256,1024]{2,1,0:T(8,128)(2,1)S(1)}, bf16[2,1024,1024]{2,1,0:T(8,128)(2,1)S(1)}, bf16[2,1024,1024]{...) custom-call(bf16[2,128,768]{2,1,0:T(8,128)(2,1)S(1)} %copy-done.6, ...), custom_call_target="tpu_custom_call" | custom-call | tf_op jit(solution)/shard_map/entry/pallas_call | solution.py:433
  94.4 2.0 copy-done.49
  98.4 2.1 fusion.66
  100.5 1.9 copy.145
  108.0 3.0 multiply_convert_fusion.1
  111.1 2.1 fusion.63.part
  115.3 15.7 %forward0.1 = (f32[32,1024]{1,0:T(8,128)S(1)}, bf16[128,1024]{1,0:T(8,128)(2,1)S(1)}) custom-call(bf16[128,1024]{1,0:T(8,128)(2,1)S(1)} %fusion.63.part, f32[32,1024]{1,0:T(8,128)S(1)} %copy-done.4, f32[1,1024]{1,0:T(1,128)S(1)} %slice.284.bias), custom_call_target="tpu_custom_call" | custom-call | tf_op jit(solution)/shard_map/forward0/pallas_call | solution.py:433
  134.0 2.8 multiply_convert_fusion
  136.9 2.5 fusion.54.refs_7_
  144.9 1.4 add.257
  146.2 2.1 fusion.69
  148.3 1.9 copy.153
  153.8 2.1 convolution_convert_fusion.1
  155.8 1.6 copy.157
  158.7 1.4 fusion.78
  163.2 2.3 fusion.155
  165.7 2.8 fusion.57.part_y
  171.4 24.7 %backward1.1 = (f32[32,1024]{1,0:T(8,128)S(1)}, f32[32,1024]{1,0:T(8,128)S(1)}, bf16[128,1024]{1,0:T(8,128)(2,1)S(1)}) custom-call(bf16[128,1024]{1,0:T(8,128)(2,1)S(1)} %copy-done.33, bf16[128,1024]{1,0:T(8,128)(2,1)S(1)} %copy-done.32, f32[32,1024]{1,0:T(8,128)S(1)} %copy-done.47, f32[1,1024]{1,0:T(1,128)S(1)} %slice.312.bias, f32[32,1024]{1,0:T(8,128)S(1)} %copy-done.22), custom_call_target="tpu_custom_call" | custom-call | tf_op jit(solution)/shard_map/backward1/pallas_call | solution.py:433
  205.0 2.9 fusion.60.refs_3_
  208.0 1.6 fusion.154
  222.3 87.8 %exit.1 = (bf16[1024,256]{1,0:T(8,128)(2,1)S(1)}, bf16[1024,1024]{1,0:T(8,128)(2,1)S(1)}, bf16[1024,768]{1,0:T(8,128)(2,1)S(1)}, bf16[1024,1024]{1,0:T(8,128)(2,...) custom-call(bf16[128,256]{1,0:T(8,128)(2,1)S(1)} %copy-done.35, ...), custom_call_target="tpu_custom_call" | custom-call | tf_op jit(solution)/shard_map/exit/pallas_call | solution.py:433
  326.5 1.6 copy.180
  331.6 2.8 convolution_bitcast_fusion.5
  (398 shorter events, 83.6 us)
Async XLA Ops:
  0.6 6.2 %copy-start.112 = (f32[2,32]{1,0:T(2,128)S(1)}, f32[2,32]{1,0:T(2,128)}, u32[]{:S(2)}) copy-start(f32[2,32]{1,0:T(2,128)} %param.16) | copy-start | bytes 772
  0.7 6.2 %copy-start.113 = (f32[2,32]{1,0:T(2,128)S(1)}, f32[2,32]{1,0:T(2,128)}, u32[]{:S(2)}) copy-start(f32[2,32]{1,0:T(2,128)} %param.17) | copy-start | bytes 772
  0.7 6.2 %copy-start.114 = (f32[2,32]{1,0:T(2,128)S(1)}, f32[2,32]{1,0:T(2,128)}, u32[]{:S(2)}) copy-start(f32[2,32]{1,0:T(2,128)} %param.18) | copy-start | bytes 772
  0.7 6.2 %copy-start.115 = (f32[2,32]{1,0:T(2,128)S(1)}, f32[2,32]{1,0:T(2,128)}, u32[]{:S(2)}) copy-start(f32[2,32]{1,0:T(2,128)} %param.19) | copy-start | bytes 772
  0.7 6.2 %copy-start.116 = (f32[2,32]{1,0:T(2,128)S(1)}, f32[2,32]{1,0:T(2,128)}, u32[]{:S(2)}) copy-start(f32[2,32]{1,0:T(2,128)} %param.20) | copy-start | bytes 772
  0.7 6.3 %copy-start.111 = (f32[2,3,32]{2,0,1:T(2,128)S(1)}, f32[2,3,32]{2,0,1:T(2,128)}, u32[]{:S(2)}) copy-start(f32[2,3,32]{2,0,1:T(2,128)} %param.22) | copy-start | bytes 2308
  0.7 6.3 %copy-start.117 = (f32[2,128]{1,0:T(2,128)S(1)}, f32[2,128]{1,0:T(2,128)}, u32[]{:S(2)}) copy-start(f32[2,128]{1,0:T(2,128)} %param.25) | copy-start | bytes 3076
  0.7 6.4 %copy-start.48 = (bf16[2,256,128]{2,1,0:T(8,128)(2,1)S(1)}, bf16[2,256,128]{2,1,0:T(8,128)(2,1)}, u32[]{:S(2)}) copy-start(bf16[2,256,128]{2,1,0:T(8,128)(2,1)} %refs_1_.1) | copy-start | bytes 393220
  98.3 5.2 %copy-start.118 = (s32[1,8]{1,0:T(1,128)S(1)}, s32[1,8]{1,0:T(1,128)}, u32[]{:S(2)}) copy-start(s32[1,8]{1,0:T(1,128)} %param.15) | copy-start | bytes 100
  103.9 7.1 %copy-start.80 = (bf16[128,4,8]{0,2,1:T(8,128)(2,1)}, bf16[128,4,8]{0,2,1:T(8,128)(2,1)S(1)}, u32[]{:S(2)}) copy-start(bf16[128,4,8]{0,2,1:T(8,128)(2,1)S(1)} %get-tuple-element.301) | copy-start | bytes 24580
  103.9 7.1 %copy-start.81 = (bf16[128,4,8]{0,2,1:T(8,128)(2,1)}, bf16[128,4,8]{0,2,1:T(8,128)(2,1)S(1)}, u32[]{:S(2)}) copy-start(bf16[128,4,8]{0,2,1:T(8,128)(2,1)S(1)} %get-tuple-element.302) | copy-start | bytes 24580
  103.9 7.1 %copy-start.82 = (bf16[128,4,8]{0,2,1:T(8,128)(2,1)}, bf16[128,4,8]{0,2,1:T(8,128)(2,1)S(1)}, u32[]{:S(2)}) copy-start(bf16[128,4,8]{0,2,1:T(8,128)(2,1)S(1)} %get-tuple-element.322) | copy-start | bytes 24580
  103.9 7.1 %copy-start.83 = (bf16[128,4,8]{0,2,1:T(8,128)(2,1)}, bf16[128,4,8]{0,2,1:T(8,128)(2,1)S(1)}, u32[]{:S(2)}) copy-start(bf16[128,4,8]{0,2,1:T(8,128)(2,1)S(1)} %get-tuple-element.323) | copy-start | bytes 24580
  104.3 6.7 %copy-start.92 = (f32[4,128]{1,0:T(4,128)}, f32[4,128]{1,0:T(4,128)S(1)}, u32[]{:S(2)}) copy-start(f32[4,128]{1,0:T(4,128)S(1)} %get-tuple-element.327) | copy-start | bytes 6148
  105.0 6.0 %copy-start.94 = (f32[4,128]{1,0:T(4,128)}, f32[4,128]{1,0:T(4,128)S(1)}, u32[]{:S(2)}) copy-start(f32[4,128]{1,0:T(4,128)S(1)} %fusion.126) | copy-start | bytes 6148
  111.1 4.2 %copy-start.4 = (f32[32,1024]{1,0:T(8,128)S(1)}, f32[32,1024]{1,0:T(8,128)}, u32[]{:S(2)}) copy-start(f32[32,1024]{1,0:T(8,128)} %refs_11_.1) | copy-start | bytes 393220
  139.4 23.7 %copy-start.27 = (bf16[128,1024]{1,0:T(8,128)(2,1)}, bf16[128,1024]{1,0:T(8,128)(2,1)S(1)}, u32[]{:S(2)}) copy-start(bf16[128,1024]{1,0:T(8,128)(2,1)S(1)} %fusion.54.refs_7_) | copy-start | bytes 786436
  143.5 7.8 %copy-start.99 = (f32[1024]{0:T(1024)}, f32[1024]{0:T(1024)S(1)}, u32[]{:S(2)}) copy-start(f32[1024]{0:T(1024)S(1)} %mul.490) | copy-start | bytes 12292
  157.4 4.1 %copy-start.68 = (bf16[128,256]{0,1:T(8,128)(2,1)S(1)}, bf16[128,256]{0,1:T(8,128)(2,1)}, u32[]{:S(2)}) copy-start(bf16[128,256]{0,1:T(8,128)(2,1)} %copy.157) | copy-start | bytes 196612
  158.7 6.8 %copy-start.70 = (bf16[4,64,128]{2,1,0:T(8,128)(2,1)}, bf16[4,64,128]{2,1,0:T(8,128)(2,1)S(1)}, u32[]{:S(2)}) copy-start(bf16[4,64,128]{2,1,0:T(8,128)(2,1)S(1)} %get-tuple-element.336) | copy-start | bytes 196612
  158.7 4.4 %copy-start.50 = (bf16[2,1024,1024]{2,1,0:T(8,128)(2,1)S(1)}, bf16[2,1024,1024]{2,1,0:T(8,128)(2,1)}, u32[]{:S(2)}) copy-start(bf16[2,1024,1024]{2,1,0:T(8,128)(2,1)} %copy-done.49) | copy-start | bytes 12582916
  165.7 34.2 %copy-start.93 = (f32[4,128]{1,0:T(4,128)S(1)}, f32[4,128]{1,0:T(4,128)}, u32[]{:S(2)}) copy-start(f32[4,128]{1,0:T(4,128)} %copy-done.92) | copy-start | bytes 6148
  196.8 12.8 %copy-start.15 = (f32[32,1024]{1,0:T(8,128)}, f32[32,1024]{1,0:T(8,128)S(1)}, u32[]{:S(2)}) copy-start(f32[32,1024]{1,0:T(8,128)S(1)} %get-tuple-element.175.refs_12_) | copy-start | bytes 393220
  199.0 5.0 %copy-start.58 = (f32[4,128,128]{1,2,0:T(8,128)S(1)}, f32[4,128,128]{1,2,0:T(8,128)}, u32[]{:S(2)}) copy-start(f32[4,128,128]{1,2,0:T(8,128)} %copy-done.57) | copy-start | bytes 786436
  (96 other events, 192.3 us)

commit v2 on v1

--- a/solution.py
+++ b/solution.py
@@ -197,44 +197,93 @@
             copy.wait_send()
 
 
-def start_dp_gather(links, items):
-    chips = links.n_dp // 2
-    core, chip = lax.rem(links.dp, 2), links.dp // 2
-    partner = links.dp + 1 - 2 * core
-    direct = []
-    for step in range(1, chips):
-        peer = lax.rem(chip + step, chips) * 2 + core
+class DpGather:
+    def __init__(self, links, items):
+        self.links = links
+        self.chips = links.n_dp // 2
+        self.core, self.chip = lax.rem(links.dp, 2), links.dp // 2
+        self.partner = links.dp + 1 - 2 * self.core
+        self.relay = self.chips == 4
+        self.whole = items
+        self.pieces = []
         for own, slot in items:
-            direct.append(links.send(own, slot(links.dp), dp=peer))
-    passed = [links.send(own, slot(links.dp), dp=partner) for own, slot in items]
-    return direct, passed
-
-
-def end_dp_gather(links, items, direct, passed):
-    chips = links.n_dp // 2
-    core, chip = lax.rem(links.dp, 2), links.dp // 2
-    partner = links.dp + 1 - 2 * core
-    position = 0
-    for step in range(1, chips):
-        origin = lax.rem(chip + chips - step, chips) * 2 + core
-        for _, slot in items:
-            direct[position].wait_recv()
-            position += 1
-            passed.append(links.send(slot(origin), slot(origin), dp=partner))
-    for copy in passed:
-        copy.wait_recv()
+            rows = own.shape[0] // 2
+            for half in range(2):
+                self.pieces.append((own, slot, pl.ds(half * rows, rows), half))
+        if self.relay:
+            near = self.chip + 1 - 2 * lax.rem(self.chip, 2)
+            far = lax.rem(self.chip + 2, 4)
+            self.across = lax.rem(near + 2, 4)
+            self.order = ((near, far), (far, near))
+            self.first = [self.out(piece, self.order[piece[3]][0]) for piece in self.pieces]
+            self.second = [self.out(piece, self.order[piece[3]][1]) for piece in self.pieces]
+        else:
+            self.direct = [
+                [self.out(piece, lax.rem(self.chip + step, self.chips)) for piece in self.pieces]
+                for step in range(1, self.chips)
+            ]
+        self.passed = [
+            links.send(own, slot(links.dp), dp=self.partner) for own, slot in items
+        ]
+        self.kept = [links.local(own, slot(links.dp)) for own, slot in items]
+
+    def device(self, chip):
+        return chip * 2 + self.core
+
+    def out(self, piece, chip):
+        own, slot, rows, _ = piece
+        return self.links.send(
+            own.at[rows], slot(self.links.dp).at[rows], dp=self.device(chip)
+        )
+
+    def pass_on(self, piece, chip, target):
+        _, slot, rows, _ = piece
+        block = slot(self.device(chip)).at[rows]
+        return self.links.send(block, block, dp=target)
+
+    def finish(self):
+        if self.relay:
+            relayed = []
+            for copy, piece in zip(self.first, self.pieces):
+                origin, target = self.order[piece[3]]
+                copy.wait_recv()
+                relayed.append(self.pass_on(piece, origin, self.device(target)))
+                self.passed.append(self.pass_on(piece, origin, self.partner))
+            for copy, piece in zip(self.second, self.pieces):
+                copy.wait_recv()
+                self.passed.append(self.pass_on(piece, self.order[piece[3]][1], self.partner))
+            for copy, piece in zip(relayed, self.pieces):
+                copy.wait_recv()
+                self.passed.append(self.pass_on(piece, self.across, self.partner))
+        else:
+            for step, copies in enumerate(self.direct):
+                origin = lax.rem(self.chip + self.chips - step - 1, self.chips)
+                for copy, piece in zip(copies, self.pieces):
+                    copy.wait_recv()
+                    self.passed.append(self.pass_on(piece, origin, self.partner))
+        for copy in self.passed:
+            copy.wait_recv()
+        for copy in self.kept:
+            copy.wait()
 
 
 def row_slot(ref, rows):
     return lambda d: ref.at[pl.ds(pl.multiple_of(d * rows, rows), rows)]
 
 
-def weight_slot(ref, layer, axis, size):
+def weight_slot(ref, axis, size):
     if axis is None:
-        return lambda d: ref.at[d, layer]
+        return lambda d: ref.at[d]
     if axis == 0:
-        return lambda d: ref.at[layer, pl.ds(pl.multiple_of(d * size, size), size), :]
-    return lambda d: ref.at[layer, :, pl.ds(pl.multiple_of(d * size, size), size)]
+        return lambda d: ref.at[pl.ds(pl.multiple_of(d * size, size), size), :]
+    return lambda d: ref.at[:, pl.ds(pl.multiple_of(d * size, size), size)]
+
+
+def weight_items(held, outs, axes):
+    return [
+        (own, weight_slot(ref, axis, own.shape[axis] if axis is not None else 0))
+        for own, ref, axis in zip(held, outs, axes)
+    ]
 
 
 def scratch_sems():
@@ -247,37 +296,26 @@
 
 def entry_kernel(n_dp, n_tensor, axes, *refs):
     n_w = len(axes)
-    w_in, (small_in, rows_in) = refs[:n_w], refs[n_w : n_w + 2]
-    w_out = refs[n_w + 2 : 2 * n_w + 2]
-    small_out, rows_out = refs[2 * n_w + 2 : 2 * n_w + 4]
-    held = refs[2 * n_w + 4 : 3 * n_w + 4]
-    links = Links(n_dp, n_tensor, *refs[3 * n_w + 4 :])
-    loads = [links.local(src, dst) for src, dst in zip(w_in, held)]
+    w_in, (small_in, x_in, d_in) = refs[:n_w], refs[n_w : n_w + 3]
+    w_out, refs = refs[n_w + 3 : 2 * n_w + 3], refs[2 * n_w + 3 :]
+    (small_out, unit_out, rows_out), refs = refs[:3], refs[3:]
+    held, refs = refs[:n_w], refs[n_w:]
+    unit_own, rows_own = refs[:2]
+    links = Links(n_dp, n_tensor, *refs[2:])
+    loads = [links.local(src.at[0], dst) for src, dst in zip(w_in, held)]
     links.barrier(True)
-    layers = w_in[0].shape[0]
+    for copy in loads:
+        copy.wait()
+    weights = DpGather(links, weight_items(held, w_out, axes))
     small_own = links.local(small_in, small_out.at[links.tensor, links.dp])
-    row_count = rows_in.shape[0]
-    slot = row_slot(rows_out, row_count)
-    rows_own = links.local(rows_in, slot(links.tensor))
-    rows_sent = [
-        links.send(rows_in, slot(links.tensor), tensor=links.tensor_peer(step))
-        for step in range(1, n_tensor)
-    ]
     small_sent = [
         links.send(small_in, small_out.at[links.tensor, links.dp], dp=links.dp_peer(step))
         for step in range(1, n_dp)
     ]
-    for copy in loads:
-        copy.wait()
-    items = []
-    for layer in range(layers):
-        for index, axis in enumerate(axes):
-            size = w_in[index].shape[1 + axis] if axis is not None else 0
-            items.append(
-                (held[index].at[layer], weight_slot(w_out[index], layer, axis, size))
-            )
-    direct, passed = start_dp_gather(links, items)
-    own = [links.local(src, slot_of(links.dp)) for src, slot_of in items]
+    unit_own[...] = unit_rows(x_in[...])[0].astype(jnp.bfloat16)
+    rows_own[...] = d_in[...].astype(jnp.bfloat16)
+    unit_sent, unit_kept = start_gather(links, unit_out, unit_own)
+    rows_sent, rows_kept = start_gather(links, rows_out, rows_own)
     small_own.wait()
     for copy in small_sent:
         copy.wait_recv()
@@ -287,12 +325,11 @@
         )
         for step in range(1, n_tensor)
     ]
-    end_dp_gather(links, items, direct, passed)
-    for copy in rows_sent + small_wide:
+    weights.finish()
+    for copy in unit_sent + rows_sent + small_wide:
         copy.wait_recv()
-    rows_own.wait()
-    for copy in own:
-        copy.wait()
+    unit_kept.wait()
+    rows_kept.wait()
     links.finish()
 
 
@@ -344,35 +381,66 @@
     )
 
 
-def forward_kernel(n_dp, n_tensor, part, resid, bias, new_resid, rows_out, landing, own, *sems):
-    links = Links(n_dp, n_tensor, *sems)
-    links.barrier(False)
-    branch = end_scatter(links, part, landing, start_scatter(links, part, landing))
+def forward_kernel(n_dp, n_tensor, axes, layer, part, resid, bias, *refs):
+    n_w = len(axes)
+    w_in, refs = refs[:n_w], refs[n_w:]
+    new_resid, rows_out = refs[:2]
+    w_out, refs = refs[2 : 2 + n_w], refs[2 + n_w :]
+    landing, own = refs[:2]
+    held, refs = refs[2 : 2 + n_w], refs[2 + n_w :]
+    links = Links(n_dp, n_tensor, *refs)
+    loads = [links.local(src.at[layer + 1], dst) for src, dst in zip(w_in, held)]
+    links.barrier(True)
+    copies = start_scatter(links, part, landing)
+    for copy in loads:
+        copy.wait()
+    weights = DpGather(links, weight_items(held, w_out, axes))
+    branch = end_scatter(links, part, landing, copies)
     values = resid[...] + branch + bias[...]
     new_resid[...] = values
     own[...] = unit_rows(values)[0].astype(jnp.bfloat16)
     copies, local = start_gather(links, rows_out, own)
+    weights.finish()
     for copy in copies:
         copy.wait_recv()
     local.wait()
     links.finish()
 
 
-def backward_kernel(
-    n_dp, n_tensor, part_y, part_e, resid, bias, dres, y_out, d_out, rows_out, land_y, land_e, own, *sems
-):
-    links = Links(n_dp, n_tensor, *sems)
-    links.barrier(False)
+def backward_kernel(n_dp, n_tensor, n_act, last, *refs):
+    acts, refs = refs[:n_act], refs[n_act:]
+    part_e, resid, dres = refs[:3]
+    refs = refs[3:]
+    if last:
+        (part_y, bias), refs = refs[:2], refs[2:]
+    act_out, refs = refs[:n_act], refs[n_act:]
+    (d_out, rows_out), refs = refs[:2], refs[2:]
+    if last:
+        y_out, refs = refs[0], refs[1:]
+    held, refs = refs[:n_act], refs[n_act:]
+    (land_e, own), refs = refs[:2], refs[2:]
+    if last:
+        land_y, refs = refs[0], refs[1:]
+    links = Links(n_dp, n_tensor, *refs)
+    loads = [links.local(src, dst) for src, dst in zip(acts, held)]
+    links.barrier(True)
     copies_e = start_scatter(links, part_e, land_e)
-    copies_y = start_scatter(links, part_y, land_y) if part_y is not None else None
+    if last:
+        copies_y = start_scatter(links, part_y, land_y)
+    for copy in loads:
+        copy.wait()
+    gathered = DpGather(
+        links, [(block, row_slot(ref, block.shape[0])) for block, ref in zip(held, act_out)]
+    )
     grad = end_scatter(links, part_e, land_e, copies_e)
     values = resid[...]
     new_d = dres[...] + back_unit(values, grad)
     d_out[...] = new_d
     own[...] = new_d.astype(jnp.bfloat16)
     copies, local = start_gather(links, rows_out, own)
-    if part_y is not None:
+    if last:
         y_out[...] = values + end_scatter(links, part_y, land_y, copies_y) + bias[...]
+    gathered.finish()
     for copy in copies:
         copy.wait_recv()
     local.wait()
@@ -399,13 +467,12 @@
     items = [
         (own, row_slot(ref, own.shape[0])) for own, ref in zip(held, act_out)
     ]
-    direct, passed = start_dp_gather(links, items)
+    gathered = DpGather(links, items)
     cross_sent = [
         links.send(cross.at[links.dp_peer(step)], cross_out.at[links.dp], dp=links.dp_peer(step))
         for step in range(1, n_dp)
     ]
-    own = [links.local(src, slot_of(links.dp)) for src, slot_of in items]
-    own.append(links.local(cross.at[links.dp], cross_out.at[links.dp]))
+    cross_kept = links.local(cross.at[links.dp], cross_out.at[links.dp])
     total = small[links.dp]
     for step, copy in enumerate(small_sent):
         copy.wait_recv()
@@ -421,11 +488,10 @@
         copy.wait_recv()
         total = total + land_t[step]
     small_out[...] = total
-    end_dp_gather(links, items, direct, passed)
+    gathered.finish()
     for copy in cross_sent:
         copy.wait_recv()
-    for copy in own:
-        copy.wait()
+    cross_kept.wait()
     links.finish()
 
 
@@ -485,11 +551,11 @@
     axes = (0, 1 if columns_ok else None, 0, 1 if columns_ok else None)
     gathered = []
     for shard, axis in zip(shards, axes):
-        shape = list(shard.shape)
+        shape = list(shard.shape[1:])
         if axis is None:
             shape = [n_dp] + shape
         else:
-            shape[1 + axis] *= n_dp
+            shape[axis] *= n_dp
         gathered.append(shaped(shape, bf16))
     smalls = (
         jnp.stack([ln1_gain, ln1_bias, ln2_gain, ln2_bias, res_bias]),
@@ -497,26 +563,29 @@
         b_fc,
     )
     packed = pack_rows(smalls)
-    unit_first = unit_rows(x_in)[0].astype(bf16)
-    rows_first = jnp.concatenate([unit_first, grad_out.astype(bf16)], axis=1)
+    unit_shape, d_shape = shaped((group_rows, width), bf16), shaped(x_in.shape, f32)
+    own_rows = pltpu.VMEM((my_rows, width), bf16)
+    land = pltpu.VMEM((n_tensor - 1, my_rows, width), bf16)
+    held = [pltpu.VMEM(shard.shape[1:], bf16) for shard in shards]
     entry = call(
         functools.partial(entry_kernel, n_dp, n_tensor, axes),
         "entry",
         0,
         tuple(gathered)
-        + (
-            shaped((n_tensor, n_dp) + packed.shape, f32),
-            shaped((group_rows, 2 * width), bf16),
-        ),
-        (ANY,) * 4 + (VMEM, VMEM),
-        [ANY] * 4 + [VMEM, VMEM],
-        [pltpu.VMEM(shard.shape, bf16) for shard in shards],
-        shards + (packed, rows_first),
-    )
-    qkv_all, out_all, fc_all, proj_all, small_all, rows_all = entry
-    if not columns_ok:
-        out_all = jnp.transpose(out_all, (1, 2, 0, 3)).reshape(layer_count, -1, width)
-        proj_all = jnp.transpose(proj_all, (1, 2, 0, 3)).reshape(layer_count, -1, width)
+        + (shaped((n_tensor, n_dp) + packed.shape, f32), unit_shape, unit_shape),
+        (ANY,) * 4 + (VMEM,) * 3,
+        [ANY] * 4 + [VMEM] * 3,
+        held + [own_rows] * 2,
+        shards + (packed, x_in, grad_out),
+    )
+    small_all, unit_full, d_rows = entry[4:]
+
+    def in_columns(matrix):
+        if matrix.ndim == 2:
+            return matrix
+        return jnp.transpose(matrix, (1, 0, 2)).reshape(-1, width)
+
+    weights = [tuple(in_columns(matrix) for matrix in entry[:4])]
     small_all = small_all.reshape(n_tensor, n_dp, -1)
     n_gain = smalls[0].size
     vectors = jnp.transpose(
@@ -537,48 +606,47 @@
 
     seq_ids, positions, row_ids = group_layout(seq_lengths[0], group_rows)
     cos_tab, sin_tab = rotary_tables(positions)
-    unit_full, d_rows = rows_all[:, :width], rows_all[:, width:]
     resid = x_in
     saved = []
     for layer in range(layer_count):
+        qkv_mat, out_mat, fc_mat, proj_mat = weights[layer]
         unit_wide = unit_full.astype(f32)
         normed_a = (unit_wide * gain_one[layer] + bias_one[layer]).astype(bf16)
         normed_m = (unit_wide * gain_two[layer] + bias_two[layer]).astype(bf16)
         projected = (
-            jnp.dot(normed_a, qkv_all[layer], preferred_element_type=f32) + qkv_vecs[layer]
+            jnp.dot(normed_a, qkv_mat, preferred_element_type=f32) + qkv_vecs[layer]
         )
         split_heads = projected.reshape(group_rows, 3, heads_here, HD)
         queries = rotate(split_heads[:, 0], cos_tab, sin_tab, 1.0).astype(bf16)
         keys = rotate(split_heads[:, 1], cos_tab, sin_tab, 1.0).astype(bf16)
         values = split_heads[:, 2].astype(bf16)
         contexts, log_totals = attention_forward(queries, keys, values, seq_ids, row_ids)
-        hidden_pre = jnp.dot(normed_m, fc_all[layer], preferred_element_type=f32) + fc_vecs[layer]
+        hidden_pre = jnp.dot(normed_m, fc_mat, preferred_element_type=f32) + fc_vecs[layer]
         activated = gelu_exact(hidden_pre).astype(bf16)
         flat_context = contexts.reshape(group_rows, -1)
         partial = (
-            jnp.dot(flat_context, out_all[layer], preferred_element_type=f32)
-            + jnp.dot(activated, proj_all[layer], preferred_element_type=f32)
+            jnp.dot(flat_context, out_mat, preferred_element_type=f32)
+            + jnp.dot(activated, proj_mat, preferred_element_type=f32)
         ).astype(bf16)
         saved.append(
             (resid, unit_full, queries, keys, values, contexts, log_totals, hidden_pre, activated)
         )
         if layer + 1 < layer_count:
-            resid, unit_full = call(
-                functools.partial(forward_kernel, n_dp, n_tensor),
+            stepped = call(
+                functools.partial(forward_kernel, n_dp, n_tensor, axes, layer),
                 f"forward{layer}",
                 1 + layer,
-                (shaped(x_in.shape, f32), shaped((group_rows, width), bf16)),
-                (VMEM, VMEM),
-                [VMEM] * 3,
-                [
-                    pltpu.VMEM((n_tensor - 1, my_rows, width), bf16),
-                    pltpu.VMEM((my_rows, width), bf16),
-                ],
-                (partial, resid, out_bias[layer][None]),
+                (d_shape, unit_shape) + tuple(gathered),
+                (VMEM,) * 2 + (ANY,) * 4,
+                [VMEM] * 3 + [ANY] * 4,
+                [land, own_rows] + held,
+                (partial, resid, out_bias[layer][None]) + shards,
             )
+            resid, unit_full = stepped[:2]
+            weights.append(tuple(in_columns(matrix) for matrix in stepped[2:]))
     d_resid = grad_out
     acts, cross, sums = [None] * layer_count, [None] * layer_count, [None] * layer_count
-    y_out = None
+    all_acts = [None] * layer_count
     for layer in reversed(range(layer_count)):
         (
             layer_input,
@@ -591,13 +659,14 @@
             hidden_pre,
             activated,
         ) = saved[layer]
+        qkv_mat, out_mat, fc_mat, proj_mat = weights[layer]
         out_bias_grad = jnp.sum(d_resid, axis=0)
         flat_context = contexts.reshape(group_rows, -1)
         transposed = (((1,), (1,)), ((), ()))
         d_context = lax.dot_general(
-            d_rows, out_all[layer], transposed, preferred_element_type=f32
+            d_rows, out_mat, transposed, preferred_element_type=f32
         ).astype(bf16)
-        d_act = lax.dot_general(d_rows, proj_all[layer], transposed, preferred_element_type=f32)
+        d_act = lax.dot_general(d_rows, proj_mat, transposed, preferred_element_type=f32)
         d_pre_b = (d_act * gelu_slope(hidden_pre)).astype(bf16)
         d_queries, d_keys, d_values = attention_backward(
             queries,
@@ -614,8 +683,8 @@
         flat_dqkv = (
             jnp.stack([d_queries, d_keys, d_values], axis=1).reshape(group_rows, -1).astype(bf16)
         )
-        d_a = lax.dot_general(flat_dqkv, qkv_all[layer], transposed, preferred_element_type=f32)
-        d_m = lax.dot_general(d_pre_b, fc_all[layer], transposed, preferred_element_type=f32)
+        d_a = lax.dot_general(flat_dqkv, qkv_mat, transposed, preferred_element_type=f32)
+        d_m = lax.dot_general(d_pre_b, fc_mat, transposed, preferred_element_type=f32)
         unit_wide = unit_full.astype(f32)
         sums[layer] = (
             jnp.sum(d_a * unit_wide, axis=0),
@@ -627,41 +696,30 @@
         part_e = (d_a * gain_one[layer] + d_m * gain_two[layer]).astype(bf16)
         acts[layer] = (flat_context, activated, flat_dqkv, d_pre_b)
         cross[layer] = jnp.stack([unit_full, d_rows]).reshape(2, group_rows, n_dp, dp_width)
-        land = pltpu.VMEM((n_tensor - 1, my_rows, width), bf16)
         if layer > 0:
             last = layer + 1 == layer_count
-            d_shape = shaped(x_in.shape, f32)
-            rows_shape = shaped((group_rows, width), bf16)
-            own = pltpu.VMEM((my_rows, width), bf16)
+            n_act = len(acts[layer])
+            stepped = call(
+                functools.partial(backward_kernel, n_dp, n_tensor, n_act, last),
+                f"backward{layer}",
+                layer_count + layer,
+                tuple(shaped((total_rows, array.shape[1]), bf16) for array in acts[layer])
+                + (d_shape, unit_shape)
+                + ((d_shape,) if last else ()),
+                (ANY,) * n_act + (VMEM,) * (3 if last else 2),
+                [ANY] * n_act + [VMEM] * (5 if last else 3),
+                [pltpu.VMEM(array.shape, bf16) for array in acts[layer]]
+                + [land, own_rows]
+                + ([land] if last else []),
+                acts[layer]
+                + (part_e, layer_input, d_resid)
+                + ((partial, out_bias[layer][None]) if last else ()),
+            )
+            all_acts[layer] = stepped[:n_act]
+            d_resid, d_rows = stepped[n_act : n_act + 2]
             if last:
-                y_out, d_resid, d_rows = call(
-                    functools.partial(backward_kernel, n_dp, n_tensor),
-                    f"backward{layer}",
-                    layer_count + layer,
-                    (d_shape, d_shape, rows_shape),
-                    (VMEM,) * 3,
-                    [VMEM] * 5,
-                    [land, land, own],
-                    (partial, part_e, layer_input, out_bias[layer][None], d_resid),
-                )
-            else:
-
-                def no_y(e, r, d, d_o, r_o, l_e, o, *sems):
-                    backward_kernel(
-                        n_dp, n_tensor, None, e, r, None, d, None, d_o, r_o, None, l_e, o, *sems
-                    )
-
-                d_resid, d_rows = call(
-                    no_y,
-                    f"backward{layer}",
-                    layer_count + layer,
-                    (d_shape, rows_shape),
-                    (VMEM,) * 2,
-                    [VMEM] * 3,
-                    [land, own],
-                    (part_e, layer_input, d_resid),
-                )
-    flat_acts = [array for group in acts for array in group]
+                y_out = stepped[n_act + 2]
+    flat_acts = acts[0]
     n_act = len(flat_acts)
     cross_in = jnp.transpose(jnp.stack(cross), (3, 0, 1, 2, 4))
     stacked = jnp.stack([jnp.stack(group) for group in sums]).reshape(-1, width)
@@ -688,12 +746,12 @@
         ],
         tuple(flat_acts) + (cross_in, small_in, part_e, layer_input, d_resid),
     )
-    all_acts, (cross_all, small_sum, grad_x) = results[:n_act], results[n_act:]
+    all_acts[0], (cross_all, small_sum, grad_x) = results[:n_act], results[n_act:]
     my_dp = lax.axis_index("dp")
     over_tokens = (((0,), (0,)), ((), ()))
     grads = [[] for _ in range(6)]
     for layer in range(layer_count):
-        context_t, act_t, dqkv_t, d_pre_t = all_acts[4 * layer : 4 * layer + 4]
+        context_t, act_t, dqkv_t, d_pre_t = all_acts[layer]
         unit_t = cross_all[:, layer, 0].reshape(total_rows, dp_width).astype(f32)
         d_t = cross_all[:, layer, 1].reshape(total_rows, dp_width)
 

time: 341 us -> 299 us (0.88)
  Pallas kernels: 211 us -> 154 us
  local copies, waits for them, and re-layouts: 63.8 us -> 81.2 us
    pallas_call x4, Pallas kernels: 211 us -> 154 us  [call(): pl.pallas_call(kernel, out_shape=outs, in_specs=in_specs, out_specs=out_s...]
    unnamed x251 -> x239, local copies, waits for them, and re-layouts: 30.7 us -> 48.9 us
where the time goes in v2:
time: 299 us; the launch traced here: 296 us
  Pallas kernels  154 us (52%)
  local copies, waits for them, and re-layouts  81.2 us (27%)
  matrix products  44.3 us (15%)
  other arithmetic  14.8 us (5%)
    pallas_call x4, Pallas kernels, call(): pl.pallas_call(kernel, out_shape=outs, in_specs=in_specs, out_specs=out_s...  154 us
    unnamed x239, local copies, waits for them, and re-layouts  48.9 us
    dot_general x8, matrix products, contract(): return lax.dot_general(left, right, over_tokens, preferred_element_type=f32)  7.33 us
    dot_general x2, matrix products, per_device(): lax.dot_general(d_rows, proj_mat, transposed, preferred_element_type=f32)  6.03 us

profile of v2, /device:TPU:1, one launch (start us, length us, event | category | flops | bytes accessed | tf_op | source)
XLA Modules:
  0.0 296.1 jit_solution(17133889458861643420)
XLA Ops:
  11.9 39.7 %entry.1 = (bf16[1024,768]{1,0:T(8,128)(2,1)S(1)}, bf16[256,1024]{1,0:T(8,128)(2,1)S(1)}, bf16[1024,1024]{1,0:T(8,128)(2,1)S(1)}, bf16[1024,1024]{1,0:T(8,128)(2...) custom-call(bf16[2,128,768]{2,1,0:T(8,128)(2,1)S(1)} %copy.144.refs_0_, ...), custom_call_target="tpu_custom_call" | custom-call | tf_op jit(solution)/shard_map/entry/pallas_call | solution.py:499
  57.0 2.5 convolution_add_fusion.5
  59.5 1.9 copy.148
  65.4 2.1 fusion.82
  74.9 34.3 %forward0.1 = (f32[32,1024]{1,0:T(8,128)S(1)}, bf16[128,1024]{1,0:T(8,128)(2,1)S(1)}, bf16[1024,768]{1,0:T(8,128)(2,1)S(1)}, bf16[256,1024]{1,0:T(8,128)(2,1)S(1...) custom-call(bf16[128,1024]{1,0:T(8,128)(2,1)S(1)} %copy-done.36, f32[32,1024]{1,0:T(8,128)S(1)} %copy-done.34, ...), custom_call_target="tpu_custom_call" | custom-call | tf_op jit(solution)/shard_map/forward0/pallas_call | solution.py:499
  109.3 1.3 copy-done.2
  111.8 1.3 copy-done.21
  118.4 1.8 convolution_add_fusion.4
  125.4 2.9 multiply_convert_fusion
  131.0 2.7 fusion.1.refs_3_
  134.4 2.2 fusion.76
  145.1 33.5 %backward1.1 = (bf16[1024,256]{1,0:T(8,128)(2,1)S(1)}, bf16[1024,1024]{1,0:T(8,128)(2,1)S(1)}, bf16[1024,768]{1,0:T(8,128)(2,1)S(1)}, bf16[1024,1024]{1,0:T(8,12...) custom-call(bf16[128,256]{1,0:T(8,128)(2,1)S(1)} %copy-done.60, ...), custom_call_target="tpu_custom_call" | custom-call | tf_op jit(solution)/shard_map/backward1/pallas_call | solution.py:499
  178.6 1.3 copy-done
  179.9 1.3 copy-done.4
  185.3 1.6 copy.183.refs_0_
  195.2 3.4 %fusion.3.refs_3_ = bf16[128,1024]{1,0:T(8,128)(2,1)} fusion(bf16[128,1024]{1,0:T(8,128)(2,1)} %copy-done.40, bf16[1024,1024]{1,0:T(8,128)(2,1)} %copy-done.19, f32[128,1024]{1,0:T(8,128)} %get-tuple-element.338), kind=kOutput, calls=%fused_computation.19 | convolution fusion | flops 269746176 | bytes 3145728 | tf_op jit(solution)/shard_map/dot_general | solution.py:669
  205.9 1.9 fusion.85
  207.9 1.4 fusion.75
  215.0 46.4 %exit.1 = (bf16[1024,256]{1,0:T(8,128)(2,1)S(1)}, bf16[1024,1024]{1,0:T(8,128)(2,1)S(1)}, bf16[1024,768]{1,0:T(8,128)(2,1)S(1)}, bf16[1024,1024]{1,0:T(8,128)(2,...) custom-call(bf16[128,256]{1,0:T(8,128)(2,1)S(1)} %copy-done.59, ...), custom_call_target="tpu_custom_call" | custom-call | tf_op jit(solution)/shard_map/exit/pallas_call | solution.py:499
  270.5 2.6 copy.187
  273.0 2.1 convolution_bitcast_fusion.4
  275.1 2.6 copy.185
  277.7 2.2 convolution_bitcast_fusion.5
  281.2 1.7 convert_reduce_fusion.3
  (381 shorter events, 99.4 us)
Async XLA Ops:
  55.0 6.5 %copy-start.37 = (bf16[128,1024]{1,0:T(8,128)(2,1)}, bf16[128,1024]{1,0:T(8,128)(2,1)S(1)}, u32[]{:S(2)}) copy-start(bf16[128,1024]{1,0:T(8,128)(2,1)S(1)} %get-tuple-element.193) | copy-start | bytes 786436
  55.2 7.3 %copy-start.114 = (s32[1,8]{1,0:T(1,128)S(1)}, s32[1,8]{1,0:T(1,128)}, u32[]{:S(2)}) copy-start(s32[1,8]{1,0:T(1,128)} %param.15) | copy-start | bytes 100
  56.1 7.5 %copy-start.100 = (f32[1024]{0:T(1024)}, f32[1024]{0:T(1024)S(1)}, u32[]{:S(2)}) copy-start(f32[1024]{0:T(1024)S(1)} %add.227) | copy-start | bytes 12292
  63.5 4.8 %copy-start.87 = (f32[128,8]{0,1:T(8,128)}, f32[128,8]{0,1:T(8,128)S(1)}, u32[]{:S(2)}) copy-start(f32[128,8]{0,1:T(8,128)S(1)} %get-tuple-element.333) | copy-start | bytes 12292
  63.5 4.8 %copy-start.88 = (bf16[128,4,8]{0,2,1:T(8,128)(2,1)}, bf16[128,4,8]{0,2,1:T(8,128)(2,1)S(1)}, u32[]{:S(2)}) copy-start(bf16[128,4,8]{0,2,1:T(8,128)(2,1)S(1)} %get-tuple-element.330) | copy-start | bytes 24580
  63.5 4.8 %copy-start.89 = (bf16[128,4,8]{0,2,1:T(8,128)(2,1)}, bf16[128,4,8]{0,2,1:T(8,128)(2,1)S(1)}, u32[]{:S(2)}) copy-start(bf16[128,4,8]{0,2,1:T(8,128)(2,1)S(1)} %get-tuple-element.331) | copy-start | bytes 24580
  63.5 4.7 %copy-start.90 = (bf16[128,4,8]{0,2,1:T(8,128)(2,1)}, bf16[128,4,8]{0,2,1:T(8,128)(2,1)S(1)}, u32[]{:S(2)}) copy-start(bf16[128,4,8]{0,2,1:T(8,128)(2,1)S(1)} %get-tuple-element.311) | copy-start | bytes 24580
  63.6 4.7 %copy-start.91 = (bf16[128,4,8]{0,2,1:T(8,128)(2,1)}, bf16[128,4,8]{0,2,1:T(8,128)(2,1)S(1)}, u32[]{:S(2)}) copy-start(bf16[128,4,8]{0,2,1:T(8,128)(2,1)S(1)} %get-tuple-element.312) | copy-start | bytes 24580
  63.7 4.6 %copy-start.106 = (pred[128,128]{0,1:T(8,128)(4,1)}, pred[128,128]{0,1:T(8,128)(4,1)S(1)}, u32[]{:S(2)}) copy-start(pred[128,128]{0,1:T(8,128)(4,1)S(1)} %fusion.60) | copy-start | bytes 49156
  64.0 4.4 %copy-start.107 = (f32[4,128]{1,0:T(4,128)}, f32[4,128]{1,0:T(4,128)S(1)}, u32[]{:S(2)}) copy-start(f32[4,128]{1,0:T(4,128)S(1)} %get-tuple-element.335) | copy-start | bytes 6148
  70.0 39.2 %copy-start.15 = (bf16[128,1024]{1,0:T(8,128)(2,1)}, bf16[128,1024]{1,0:T(8,128)(2,1)S(1)}, u32[]{:S(2)}) copy-start(bf16[128,1024]{1,0:T(8,128)(2,1)S(1)} %get-tuple-element.337.refs_1_) | copy-start | bytes 786436
  117.6 16.7 %copy-start.84 = (f32[1024]{0:T(1024)}, f32[1024]{0:T(1024)S(1)}, u32[]{:S(2)}) copy-start(f32[1024]{0:T(1024)S(1)} %mul.247) | copy-start | bytes 12292
  120.2 4.5 %copy-start.81 = (f32[1,1,8,4,32]{4,1,0,2,3:T(1,128)S(1)}, f32[1,1,8,4,32]{4,1,0,2,3:T(1,128)}, u32[]{:S(2)}) copy-start(f32[1,1,8,4,32]{4,1,0,2,3:T(1,128)} %get-tuple-element.291) | copy-start | bytes 12292
  120.4 4.3 %copy-start.71 = (f32[128,768]{0,1:T(8,128)}, f32[128,768]{0,1:T(8,128)S(1)}, u32[]{:S(2)}) copy-start(f32[128,768]{0,1:T(8,128)S(1)} %copy.157) | copy-start | bytes 1179652
  125.3 9.1 %copy-start.83 = (f32[1024]{0:T(1024)}, f32[1024]{0:T(1024)S(1)}, u32[]{:S(2)}) copy-start(f32[1024]{0:T(1024)S(1)} %mul.488) | copy-start | bytes 12292
  125.3 4.4 %copy-start.97 = (bf16[128,4,8]{0,2,1:T(8,128)(2,1)S(1)}, bf16[128,4,8]{0,2,1:T(8,128)(2,1)}, u32[]{:S(2)}) copy-start(bf16[128,4,8]{0,2,1:T(8,128)(2,1)} %copy-done.96) | copy-start | bytes 24580
  125.3 4.4 %copy-start.99 = (bf16[128,4,8]{0,2,1:T(8,128)(2,1)S(1)}, bf16[128,4,8]{0,2,1:T(8,128)(2,1)}, u32[]{:S(2)}) copy-start(bf16[128,4,8]{0,2,1:T(8,128)(2,1)} %copy-done.98) | copy-start | bytes 24580
  125.3 4.5 %copy-start.78 = (bf16[128,4,48]{0,2,1:T(8,128)(2,1)S(1)}, bf16[128,4,48]{0,2,1:T(8,128)(2,1)}, u32[]{:S(2)}) copy-start(bf16[128,4,48]{0,2,1:T(8,128)(2,1)} %copy-done.77) | copy-start | bytes 147460
  125.3 4.5 %copy-start.93 = (bf16[128,4,8]{0,2,1:T(8,128)(2,1)S(1)}, bf16[128,4,8]{0,2,1:T(8,128)(2,1)}, u32[]{:S(2)}) copy-start(bf16[128,4,8]{0,2,1:T(8,128)(2,1)} %copy-done.92) | copy-start | bytes 24580
  125.3 4.5 %copy-start.95 = (bf16[128,4,8]{0,2,1:T(8,128)(2,1)S(1)}, bf16[128,4,8]{0,2,1:T(8,128)(2,1)}, u32[]{:S(2)}) copy-start(bf16[128,4,8]{0,2,1:T(8,128)(2,1)} %copy-done.94) | copy-start | bytes 24580
  125.3 4.7 %copy-start.85 = (f32[128,8]{0,1:T(8,128)S(1)}, f32[128,8]{0,1:T(8,128)}, u32[]{:S(2)}) copy-start(f32[128,8]{0,1:T(8,128)} %get-tuple-element.332) | copy-start | bytes 12292
  136.9 49.9 %copy-start.28 = (bf16[256,1024]{1,0:T(8,128)(2,1)S(1)}, bf16[256,1024]{1,0:T(8,128)(2,1)}, u32[]{:S(2)}) copy-start(bf16[256,1024]{1,0:T(8,128)(2,1)} %copy-done.27) | copy-start | bytes 1572868
  185.3 8.9 %copy-start.86 = (f32[128,8]{0,1:T(8,128)S(1)}, f32[128,8]{0,1:T(8,128)}, u32[]{:S(2)}) copy-start(f32[128,8]{0,1:T(8,128)} %get-tuple-element.332) | copy-start | bytes 12292
  195.2 5.4 %copy-start.41 = (bf16[128,1024]{1,0:T(8,128)(2,1)S(1)}, bf16[128,1024]{1,0:T(8,128)(2,1)}, u32[]{:S(2)}) copy-start(bf16[128,1024]{1,0:T(8,128)(2,1)} %copy-done.40) | copy-start | bytes 786436
  (91 other events, 151.4 us)

commit v3 on v2

--- a/solution.py
+++ b/solution.py
@@ -41,96 +41,6 @@
     inverse = jnp.power(10000.0, -2.0 * freq_ids / ROT)
     angles = positions.astype(jnp.float32)[:, None] * inverse[None, :]
     return (jnp.cos(angles), jnp.sin(angles))
-
-
-def rotate(vectors, cos_tab, sin_tab, direction_sign):
-    half_rot = ROT // 2
-    lower_half = vectors[..., :half_rot]
-    upper_half = vectors[..., half_rot:ROT]
-    cos_b = cos_tab[:, None, :]
-    sin_b = sin_tab[:, None, :]
-    new_lower = lower_half * cos_b - direction_sign * upper_half * sin_b
-    new_upper = upper_half * cos_b + direction_sign * lower_half * sin_b
-    return jnp.concatenate([new_lower, new_upper, vectors[..., ROT:]], axis=-1)
-
-
-def masked_block(q_blk, keys, q_seq, q_row, seq_ids, row_ids):
-    scores = jnp.einsum("qhd,khd->hqk", q_blk, keys, preferred_element_type=jnp.float32) * HD ** (
-        -0.5
-    )
-    allowed = (q_seq[:, None] == seq_ids[None, :]) & (row_ids[None, :] <= q_row[:, None])
-    return jnp.where(allowed[None], scores, NEG_FILL)
-
-
-def attention_forward(queries, keys, values, seq_ids, row_ids):
-    total_rows, heads_here, head_dim = queries.shape
-    block_rows = min(512, total_rows)
-    blocks = total_rows // block_rows
-
-    def one_block(inputs):
-        q_blk, q_seq, q_row = inputs
-        scores = masked_block(q_blk, keys, q_seq, q_row, seq_ids, row_ids)
-        top_val = jnp.max(scores, axis=-1, keepdims=True)
-        exponent_terms = jnp.exp(scores - top_val)
-        totals = jnp.sum(exponent_terms, axis=-1, keepdims=True)
-        attn_probs = (exponent_terms / totals).astype(jnp.bfloat16)
-        context = jnp.einsum(
-            "hqk,khd->qhd", attn_probs, values, preferred_element_type=jnp.float32
-        ).astype(jnp.bfloat16)
-        return (context, (top_val + jnp.log(totals))[..., 0])
-
-    contexts, log_totals = lax.map(
-        one_block,
-        (
-            queries.reshape(blocks, block_rows, heads_here, head_dim),
-            seq_ids.reshape(blocks, block_rows),
-            row_ids.reshape(blocks, block_rows),
-        ),
-    )
-    return (contexts.reshape(total_rows, heads_here, head_dim), log_totals)
-
-
-def attention_backward(queries, keys, values, contexts, d_context, log_totals, seq_ids, row_ids):
-    total_rows, heads_here, head_dim = queries.shape
-    block_rows = min(512, total_rows)
-    blocks = total_rows // block_rows
-
-    def one_block(carry, inputs):
-        d_keys, d_values = carry
-        q_blk, c_blk, dc_blk, lse_blk, q_seq, q_row = inputs
-        scores = masked_block(q_blk, keys, q_seq, q_row, seq_ids, row_ids)
-        probs_full = jnp.exp(scores - lse_blk[..., None])
-        d_probs = jnp.einsum("qhd,khd->hqk", dc_blk, values, preferred_element_type=jnp.float32)
-        delta = jnp.sum(dc_blk.astype(jnp.float32) * c_blk.astype(jnp.float32), axis=-1)
-        d_scores = probs_full * (d_probs - jnp.transpose(delta)[:, :, None])
-        d_scaled = (d_scores * HD ** (-0.5)).astype(jnp.bfloat16)
-        d_q = jnp.einsum("hqk,khd->qhd", d_scaled, keys, preferred_element_type=jnp.float32)
-        d_keys = d_keys + jnp.einsum(
-            "hqk,qhd->khd", d_scaled, q_blk, preferred_element_type=jnp.float32
-        )
-        d_values = d_values + jnp.einsum(
-            "hqk,qhd->khd",
-            probs_full.astype(jnp.bfloat16),
-            dc_blk,
-            preferred_element_type=jnp.float32,
-        )
-        return ((d_keys, d_values), d_q)
-
-    zero_keys = jnp.zeros(keys.shape, jnp.float32)
-    shape_blk = (blocks, block_rows, heads_here, head_dim)
-    carry_out, d_queries = lax.scan(
-        one_block,
-        (zero_keys, zero_keys),
-        (
-            queries.reshape(shape_blk),
-            contexts.reshape(shape_blk),
-            d_context.reshape(shape_blk),
-            log_totals,
-            seq_ids.reshape(blocks, block_rows),
-            row_ids.reshape(blocks, block_rows),
-        ),
-    )
-    return (d_queries.reshape(total_rows, heads_here, head_dim), carry_out[0], carry_out[1])
 
 
 MESH = pl.DeviceIdType.MESH
@@ -495,6 +405,134 @@
     links.finish()
 
 
+def dot_nn(left, right):
+    return jnp.dot(left, right, preferred_element_type=jnp.float32)
+
+
+def dot_nt(left, right):
+    return lax.dot_general(left, right, (((1,), (1,)), ((), ())), preferred_element_type=jnp.float32)
+
+
+def dot_tn(left, right):
+    return lax.dot_general(left, right, (((0,), (0,)), ((), ())), preferred_element_type=jnp.float32)
+
+
+def turn(vectors, same, up, down, sign):
+    width = vectors.shape[1]
+    above = pltpu.roll(vectors, width - ROT // 2, 1)
+    below = pltpu.roll(vectors, ROT // 2, 1)
+    return vectors * same + sign * (above * up + below * down)
+
+
+def head_scores(query, key, mask):
+    scores = dot_nt(query, key) * HD ** (-0.5)
+    scores = jnp.where(mask, scores, NEG_FILL)
+    terms = jnp.exp(scores - jnp.max(scores, axis=-1, keepdims=True))
+    return terms / jnp.sum(terms, axis=-1, keepdims=True)
+
+
+def forward_math(
+    unit, g1, b1, g2, b2, qkv_mat, qkv_vec, out_mat, fc_mat, fc_vec, proj_mat, mask, same, up, down,
+    qkv_out, ctx_out, pre_out, act_out, part_out,
+):
+    bf16 = jnp.bfloat16
+    wide = unit[...].astype(jnp.float32)
+    normed_a = (wide * g1[...] + b1[...]).astype(bf16)
+    normed_m = (wide * g2[...] + b2[...]).astype(bf16)
+    projected = dot_nn(normed_a, qkv_mat[...]) + qkv_vec[...]
+    part = ctx_out.shape[1]
+    tables = (same[...], up[...], down[...])
+    for which in range(3):
+        block = projected[:, which * part : (which + 1) * part]
+        if which < 2:
+            block = turn(block, *tables, 1.0)
+        qkv_out[:, which * part : (which + 1) * part] = block.astype(bf16)
+    allowed = mask[...] > 0.0
+    for head in range(part // HD):
+        q, k, v = (
+            qkv_out[:, which * part + head * HD : which * part + (head + 1) * HD]
+            for which in range(3)
+        )
+        probs = head_scores(q, k, allowed).astype(bf16)
+        ctx_out[:, head * HD : (head + 1) * HD] = dot_nn(probs, v).astype(bf16)
+    hidden = dot_nn(normed_m, fc_mat[...]) + fc_vec[...]
+    pre_out[...] = hidden
+    act_out[...] = gelu_exact(hidden).astype(bf16)
+    part_out[...] = (dot_nn(ctx_out[...], out_mat[...]) + dot_nn(act_out[...], proj_mat[...])).astype(
+        bf16
+    )
+
+
+def backward_math(
+    unit, g1, g2, qkv_mat, out_mat, fc_mat, proj_mat, mask, same, up, down, d_rows, qkv, ctx, pre,
+    dqkv_out, du_out, part_out, sums_out, d_ctx,
+):
+    bf16, f32 = jnp.bfloat16, jnp.float32
+    d_ctx[...] = dot_nt(d_rows[...], out_mat[...]).astype(bf16)
+    du_out[...] = (dot_nt(d_rows[...], proj_mat[...]) * gelu_slope(pre[...])).astype(bf16)
+    part = ctx.shape[1]
+    allowed = mask[...] > 0.0
+    pieces = [[], [], []]
+    for head in range(part // HD):
+        here = slice(head * HD, (head + 1) * HD)
+        q, k, v = (
+            qkv[:, which * part + head * HD : which * part + (head + 1) * HD] for which in range(3)
+        )
+        dc = d_ctx[:, here]
+        probs = head_scores(q, k, allowed)
+        delta = jnp.sum(dc.astype(f32) * ctx[:, here].astype(f32), axis=-1, keepdims=True)
+        d_scaled = (probs * (dot_nt(dc, v) - delta) * HD ** (-0.5)).astype(bf16)
+        pieces[0].append(dot_nn(d_scaled, k))
+        pieces[1].append(dot_tn(d_scaled, q))
+        pieces[2].append(dot_tn(probs.astype(bf16), dc))
+    tables = (same[...], up[...], down[...])
+    for which in range(3):
+        block = jnp.concatenate(pieces[which], axis=1)
+        if which < 2:
+            block = turn(block, *tables, -1.0)
+        dqkv_out[:, which * part : (which + 1) * part] = block.astype(bf16)
+    d_a = dot_nt(dqkv_out[...], qkv_mat[...])
+    d_m = dot_nt(du_out[...], fc_mat[...])
+    wide = unit[...].astype(f32)
+    sums_out[0:1] = jnp.sum(d_a * wide, axis=0, keepdims=True)
+    sums_out[1:2] = jnp.sum(d_a, axis=0, keepdims=True)
+    sums_out[2:3] = jnp.sum(d_m * wide, axis=0, keepdims=True)
+    sums_out[3:4] = jnp.sum(d_m, axis=0, keepdims=True)
+    part_out[...] = (d_a * g1[...] + d_m * g2[...]).astype(bf16)
+
+
+def weight_grads_math(layers, cross, *refs):
+    vectors, refs = refs[0], refs[1:]
+    acts, (qkv_g, out_g, fc_g, proj_g, qkv_s, fc_s) = refs[: 4 * layers], refs[4 * layers :]
+    bf16, f32 = jnp.bfloat16, jnp.float32
+    width = cross.shape[-1]
+    for layer in range(layers):
+        context, act, dqkv, d_pre = acts[4 * layer : 4 * layer + 4]
+        unit = cross[:, layer, 0].reshape(-1, width).astype(f32)
+        d_t = cross[:, layer, 1].reshape(-1, width)
+        g1, b1, g2, b2 = (vectors[layer, row : row + 1] for row in range(4))
+        a_t = (unit * g1 + b1).astype(bf16)
+        m_t = (unit * g2 + b2).astype(bf16)
+        qkv_g[layer] = dot_tn(a_t, dqkv[...])
+        fc_g[layer] = dot_tn(m_t, d_pre[...])
+        out_g[layer] = jnp.transpose(dot_tn(d_t, context[...]))
+        proj_g[layer] = jnp.transpose(dot_tn(d_t, act[...]))
+        qkv_s[layer : layer + 1] = jnp.sum(dqkv[...].astype(f32), axis=0, keepdims=True)
+        fc_s[layer : layer + 1] = jnp.sum(d_pre[...].astype(f32), axis=0, keepdims=True)
+
+
+def plain(kernel, name, outs, scratch, args):
+    return pl.pallas_call(
+        kernel,
+        out_shape=outs,
+        in_specs=[VMEM] * len(args),
+        out_specs=(VMEM,) * len(outs),
+        scratch_shapes=scratch,
+        name=name,
+        compiler_params=pltpu.CompilerParams(vmem_limit_bytes=40 << 20),
+    )(*args)
+
+
 def call(kernel, name, collective, outs, out_specs, in_specs, scratch, args):
     return pl.pallas_call(
         kernel,
@@ -606,31 +644,40 @@
 
     seq_ids, positions, row_ids = group_layout(seq_lengths[0], group_rows)
     cos_tab, sin_tab = rotary_tables(positions)
+    flat = jnp.zeros((group_rows, HD - ROT), f32)
+    none = jnp.zeros_like(sin_tab)
+    same = jnp.tile(jnp.concatenate([cos_tab, cos_tab, flat + 1.0], axis=1), (1, heads_here))
+    up = jnp.tile(jnp.concatenate([-sin_tab, none, flat], axis=1), (1, heads_here))
+    down = jnp.tile(jnp.concatenate([none, sin_tab, flat], axis=1), (1, heads_here))
+    mask = (
+        (seq_ids[:, None] == seq_ids[None, :]) & (row_ids[None, :] <= row_ids[:, None])
+    ).astype(f32)
+    tables = (mask, same, up, down)
+    part_width = heads_here * HD
     resid = x_in
     saved = []
     for layer in range(layer_count):
         qkv_mat, out_mat, fc_mat, proj_mat = weights[layer]
-        unit_wide = unit_full.astype(f32)
-        normed_a = (unit_wide * gain_one[layer] + bias_one[layer]).astype(bf16)
-        normed_m = (unit_wide * gain_two[layer] + bias_two[layer]).astype(bf16)
-        projected = (
-            jnp.dot(normed_a, qkv_mat, preferred_element_type=f32) + qkv_vecs[layer]
-        )
-        split_heads = projected.reshape(group_rows, 3, heads_here, HD)
-        queries = rotate(split_heads[:, 0], cos_tab, sin_tab, 1.0).astype(bf16)
-        keys = rotate(split_heads[:, 1], cos_tab, sin_tab, 1.0).astype(bf16)
-        values = split_heads[:, 2].astype(bf16)
-        contexts, log_totals = attention_forward(queries, keys, values, seq_ids, row_ids)
-        hidden_pre = jnp.dot(normed_m, fc_mat, preferred_element_type=f32) + fc_vecs[layer]
-        activated = gelu_exact(hidden_pre).astype(bf16)
-        flat_context = contexts.reshape(group_rows, -1)
-        partial = (
-            jnp.dot(flat_context, out_mat, preferred_element_type=f32)
-            + jnp.dot(activated, proj_mat, preferred_element_type=f32)
-        ).astype(bf16)
-        saved.append(
-            (resid, unit_full, queries, keys, values, contexts, log_totals, hidden_pre, activated)
-        )
+        gains = tuple(
+            vector[layer][None] for vector in (gain_one, bias_one, gain_two, bias_two)
+        )
+        qkv_flat, flat_context, hidden_pre, activated, partial = plain(
+            forward_math,
+            f"math_forward{layer}",
+            (
+                shaped((group_rows, 3 * part_width), bf16),
+                shaped((group_rows, part_width), bf16),
+                shaped((group_rows, fc_mat.shape[1]), f32),
+                shaped((group_rows, fc_mat.shape[1]), bf16),
+                unit_shape,
+            ),
+            [],
+            (unit_full,)
+            + gains
+            + (qkv_mat, qkv_vecs[layer], out_mat, fc_mat, fc_vecs[layer], proj_mat)
+            + tables,
+        )
+        saved.append((resid, unit_full, qkv_flat, flat_context, hidden_pre, activated, gains))
         if layer + 1 < layer_count:
             stepped = call(
                 functools.partial(forward_kernel, n_dp, n_tensor, axes, layer),
@@ -648,52 +695,23 @@
     acts, cross, sums = [None] * layer_count, [None] * layer_count, [None] * layer_count
     all_acts = [None] * layer_count
     for layer in reversed(range(layer_count)):
-        (
-            layer_input,
-            unit_full,
-            queries,
-            keys,
-            values,
-            contexts,
-            log_totals,
-            hidden_pre,
-            activated,
-        ) = saved[layer]
+        layer_input, unit_full, qkv_flat, flat_context, hidden_pre, activated, gains = saved[layer]
         qkv_mat, out_mat, fc_mat, proj_mat = weights[layer]
-        out_bias_grad = jnp.sum(d_resid, axis=0)
-        flat_context = contexts.reshape(group_rows, -1)
-        transposed = (((1,), (1,)), ((), ()))
-        d_context = lax.dot_general(
-            d_rows, out_mat, transposed, preferred_element_type=f32
-        ).astype(bf16)
-        d_act = lax.dot_general(d_rows, proj_mat, transposed, preferred_element_type=f32)
-        d_pre_b = (d_act * gelu_slope(hidden_pre)).astype(bf16)
-        d_queries, d_keys, d_values = attention_backward(
-            queries,
-            keys,
-            values,
-            contexts,
-            d_context.reshape(group_rows, heads_here, HD),
-            log_totals,
-            seq_ids,
-            row_ids,
-        )
-        d_queries = rotate(d_queries, cos_tab, sin_tab, -1.0)
-        d_keys = rotate(d_keys, cos_tab, sin_tab, -1.0)
-        flat_dqkv = (
-            jnp.stack([d_queries, d_keys, d_values], axis=1).reshape(group_rows, -1).astype(bf16)
-        )
-        d_a = lax.dot_general(flat_dqkv, qkv_mat, transposed, preferred_element_type=f32)
-        d_m = lax.dot_general(d_pre_b, fc_mat, transposed, preferred_element_type=f32)
-        unit_wide = unit_full.astype(f32)
-        sums[layer] = (
-            jnp.sum(d_a * unit_wide, axis=0),
-            jnp.sum(d_a, axis=0),
-            jnp.sum(d_m * unit_wide, axis=0),
-            jnp.sum(d_m, axis=0),
-            out_bias_grad,
-        )
-        part_e = (d_a * gain_one[layer] + d_m * gain_two[layer]).astype(bf16)
+        flat_dqkv, d_pre_b, part_e, vector_sums = plain(
+            backward_math,
+            f"math_backward{layer}",
+            (
+                shaped(qkv_flat.shape, bf16),
+                shaped(activated.shape, bf16),
+                unit_shape,
+                shaped((4, width), f32),
+            ),
+            [pltpu.VMEM((group_rows, part_width), bf16)],
+            (unit_full, gains[0], gains[2], qkv_mat, out_mat, fc_mat, proj_mat)
+            + tables
+            + (d_rows, qkv_flat, flat_context, hidden_pre),
+        )
+        sums[layer] = jnp.concatenate([vector_sums, jnp.sum(d_resid, axis=0)[None]])
         acts[layer] = (flat_context, activated, flat_dqkv, d_pre_b)
         cross[layer] = jnp.stack([unit_full, d_rows]).reshape(2, group_rows, n_dp, dp_width)
         if layer > 0:
@@ -722,7 +740,7 @@
     flat_acts = acts[0]
     n_act = len(flat_acts)
     cross_in = jnp.transpose(jnp.stack(cross), (3, 0, 1, 2, 4))
-    stacked = jnp.stack([jnp.stack(group) for group in sums]).reshape(-1, width)
+    stacked = jnp.stack(sums).reshape(-1, width)
     n_sums = stacked.shape[0]
     padded = -(-n_sums // 8) * 8
     small_in = jnp.transpose(
@@ -748,33 +766,62 @@
     )
     all_acts[0], (cross_all, small_sum, grad_x) = results[:n_act], results[n_act:]
     my_dp = lax.axis_index("dp")
-    over_tokens = (((0,), (0,)), ((), ()))
-    grads = [[] for _ in range(6)]
-    for layer in range(layer_count):
-        context_t, act_t, dqkv_t, d_pre_t = all_acts[layer]
-        unit_t = cross_all[:, layer, 0].reshape(total_rows, dp_width).astype(f32)
-        d_t = cross_all[:, layer, 1].reshape(total_rows, dp_width)
-
-        def here(vector):
-            return lax.dynamic_slice_in_dim(vector[layer], my_dp * dp_width, dp_width)
-
-        a_t = (unit_t * here(gain_one) + here(bias_one)).astype(bf16)
-        m_t = (unit_t * here(gain_two) + here(bias_two)).astype(bf16)
-
-        def contract(left, right):
-            return lax.dot_general(left, right, over_tokens, preferred_element_type=f32)
-
-        qkv_sums = jnp.sum(dqkv_t.astype(f32), axis=0).reshape(3, -1)
-        fc_sums = jnp.sum(d_pre_t.astype(f32), axis=0)
-        grads[0].append(contract(a_t, dqkv_t).reshape(w_qkv.shape[1:]))
-        grads[1].append(
-            lax.dynamic_slice_in_dim(qkv_sums, my_dp * b_qkv.shape[2], b_qkv.shape[2], axis=1)
-        )
-        grads[2].append(contract(context_t, d_t))
-        grads[3].append(contract(m_t, d_pre_t))
-        grads[4].append(lax.dynamic_slice_in_dim(fc_sums, my_dp * b_fc.shape[1], b_fc.shape[1]))
-        grads[5].append(contract(act_t, d_t))
-    stacked_grads = tuple(jnp.stack(group) for group in grads)
+    in_vmem = total_rows * sum(array.shape[1] for array in acts[0]) * 2 * layer_count <= 16 << 20
+    if in_vmem and columns_ok:
+        vectors = jnp.transpose(jnp.stack([gain_one, bias_one, gain_two, bias_two]), (1, 0, 2))
+        vectors = lax.dynamic_slice_in_dim(vectors, my_dp * dp_width, dp_width, axis=2)
+        flat_qkv, out_g, fc_g, proj_g, qkv_s, fc_s = plain(
+            functools.partial(weight_grads_math, layer_count),
+            "math_grads",
+            (
+                shaped((layer_count, dp_width, 3 * part_width), f32),
+                shaped(w_out.shape, f32),
+                shaped(w_fc.shape, f32),
+                shaped(w_proj.shape, f32),
+                shaped((layer_count, 3 * part_width), f32),
+                shaped((layer_count, w_fc.shape[2]), f32),
+            ),
+            [],
+            (cross_all, vectors) + tuple(array for group in all_acts for array in group),
+        )
+        stacked_grads = (
+            flat_qkv.reshape(w_qkv.shape),
+            lax.dynamic_slice_in_dim(
+                qkv_s.reshape(layer_count, 3, -1), my_dp * b_qkv.shape[2], b_qkv.shape[2], axis=2
+            ),
+            out_g,
+            fc_g,
+            lax.dynamic_slice_in_dim(fc_s, my_dp * b_fc.shape[1], b_fc.shape[1], axis=1),
+            proj_g,
+        )
+    else:
+        over_tokens = (((0,), (0,)), ((), ()))
+        grads = [[] for _ in range(6)]
+        for layer in range(layer_count):
+            context_t, act_t, dqkv_t, d_pre_t = all_acts[layer]
+            unit_t = cross_all[:, layer, 0].reshape(total_rows, dp_width).astype(f32)
+            d_t = cross_all[:, layer, 1].reshape(total_rows, dp_width)
+
+            def here(vector):
+                return lax.dynamic_slice_in_dim(vector[layer], my_dp * dp_width, dp_width)
+
+            a_t = (unit_t * here(gain_one) + here(bias_one)).astype(bf16)
+            m_t = (unit_t * here(gain_two) + here(bias_two)).astype(bf16)
+
+            def contract(left, right):
+                return lax.dot_general(left, right, over_tokens, preferred_element_type=f32)
+
+            qkv_sums = jnp.sum(dqkv_t.astype(f32), axis=0).reshape(3, -1)
+            fc_sums = jnp.sum(d_pre_t.astype(f32), axis=0)
+            grads[0].append(contract(a_t, dqkv_t).reshape(w_qkv.shape[1:]))
+            grads[1].append(
+                lax.dynamic_slice_in_dim(qkv_sums, my_dp * b_qkv.shape[2], b_qkv.shape[2], axis=1)
+            )
+            grads[2].append(contract(context_t, d_t))
+            grads[3].append(contract(m_t, d_pre_t))
+            grads[4].append(lax.dynamic_slice_in_dim(fc_sums, my_dp * b_fc.shape[1], b_fc.shape[1]))
+            grads[5].append(contract(act_t, d_t))
+        stacked_grads = tuple(jnp.stack(group) for group in grads)
     vector_grads = lax.dynamic_slice_in_dim(
         small_sum[:n_sums].reshape(layer_count, 5, dp_width), my_tensor * vec_width, vec_width, axis=2
     )

time: 299 us -> 277 us (0.926)
  matrix products: 44.3 us -> 0 us
  local copies, waits for them, and re-layouts: 81.2 us -> 99.1 us
  Pallas kernels: 154 us -> 170 us
  other arithmetic: 14.8 us -> 3.92 us
    dot_general x36 -> x0, matrix products: 44.3 us -> none  [the longest x8 7.33 us: contract(): return lax.dot_general(left, right, over_tokens, preferred_element_type=f32)]
    unnamed x239 -> x198, local copies, waits for them, and re-layouts: 48.9 us -> 82.3 us
    pallas_call x0 -> x5, Pallas kernels: none -> 16.1 us  [plain(): pl.pallas_call(kernel, out_shape=outs, in_specs=[VMEM] * len(args), out_s...]
    dot_general x2 -> x0, local copies, waits for them, and re-layouts: 5.16 us -> none  [contract(): return lax.dot_general(left, right, over_tokens, preferred_element_type=f32)]
    dynamic_slice x8 -> x2, local copies, waits for them, and re-layouts: 4.63 us -> 0.64 us  [the longest x1 0.56 us: per_device(): lax.dynamic_slice_in_dim(fc_s, my_dp * b_fc.shape[1], b_fc.shape[1], axis=1)]
    another operation x17 -> x4, other arithmetic: 5.37 us -> 1.65 us  [the longest x3 1.47 us: per_device(): stacked = jnp.stack(sums).reshape(-1, width)]
    reduce_sum x9 -> x2, other arithmetic: 4.34 us -> 0.94 us  [per_device(): sums[layer] = jnp.concatenate([vector_sums, jnp.sum(d_resid, axis=0)[None]])]
    add x9 -> x1, local copies, waits for them, and re-layouts: 3.15 us -> 0.01 us  [per_device(): flat + 1.0]
where the time goes in v3:
time: 277 us; the launch traced here: 274 us
  Pallas kernels  170 us (61%)
  local copies, waits for them, and re-layouts  99.1 us (36%)
  other arithmetic  3.92 us (1%)
    pallas_call x4, Pallas kernels, call(): pl.pallas_call(kernel, out_shape=outs, in_specs=in_specs, out_specs=out_s...  154 us
    unnamed x198, local copies, waits for them, and re-layouts  82.3 us
    pallas_call x5, Pallas kernels, plain(): pl.pallas_call(kernel, out_shape=outs, in_specs=[VMEM] * len(args), out_s...  16.1 us

profile of v3, /device:TPU:1, one launch (start us, length us, event | category | flops | bytes accessed | tf_op | source)
XLA Modules:
  0.0 274.4 jit_solution(14791643753817076723)
XLA Ops:
  11.9 39.7 %entry.1 = (bf16[1024,768]{1,0:T(8,128)(2,1)S(1)}, bf16[256,1024]{1,0:T(8,128)(2,1)S(1)}, bf16[1024,1024]{1,0:T(8,128)(2,1)S(1)}, bf16[1024,1024]{1,0:T(8,128)(2...) custom-call(bf16[2,128,768]{2,1,0:T(8,128)(2,1)S(1)} %copy.77.refs_0_, ...), custom_call_target="tpu_custom_call" | custom-call | tf_op jit(solution)/shard_map/entry/pallas_call | solution.py:537
  59.6 1.6 copy-done.1
  61.2 1.4 copy-done.9
  64.4 2.3 math_forward0.1
  74.5 34.3 %forward0.1 = (f32[32,1024]{1,0:T(8,128)S(1)}, bf16[128,1024]{1,0:T(8,128)(2,1)S(1)}, bf16[1024,768]{1,0:T(8,128)(2,1)S(1)}, bf16[256,1024]{1,0:T(8,128)(2,1)S(1...) custom-call(bf16[128,1024]{1,0:T(8,128)(2,1)S(1)} %copy-done.65, f32[32,1024]{1,0:T(8,128)S(1)} %copy-done.38, ...), custom_call_target="tpu_custom_call" | custom-call | tf_op jit(solution)/shard_map/forward0/pallas_call | solution.py:537
  108.8 1.3 copy-done.3
  118.2 1.6 copy-done.4
  119.8 1.6 copy-done.7
  121.4 1.4 copy-done.12
  124.5 2.3 math_forward1.1
  126.9 4.0 %math_backward1.1 = (bf16[128,768]{1,0:T(8,128)(2,1)S(1)}, bf16[128,1024]{1,0:T(8,128)(2,1)S(1)}, bf16[128,1024]{1,0:T(8,128)(2,1)S(1)}, f32[4,1024]{1,0:T(4,128)S(1)}) custom-call(bf16[128,1024]{1,0:T(8,128)(2,1)S(1)} %get-tuple-element.71.unit, f32[1,1024]{1,0:T(1,128)S(1)} %slice.134.g1, f32[1,1024]{1,0:T(1,128)S(1)} %slice.138.g2, ...), custom_call_target="tpu_custom_call" | custom-call | tf_op jit(solution)/shard_map/math_backward1/pallas_call | solution.py:525
  141.6 33.5 %backward1.1 = (bf16[1024,256]{1,0:T(8,128)(2,1)S(1)}, bf16[1024,1024]{1,0:T(8,128)(2,1)S(1)}, bf16[1024,768]{1,0:T(8,128)(2,1)S(1)}, bf16[1024,1024]{1,0:T(8,12...) custom-call(bf16[128,256]{1,0:T(8,128)(2,1)S(1)} %copy-done.57, ...), custom_call_target="tpu_custom_call" | custom-call | tf_op jit(solution)/shard_map/backward1/pallas_call | solution.py:537
  175.1 1.3 copy-done.14
  177.8 2.5 copy-done.2
  183.3 4.0 %math_backward0.1 = (bf16[128,768]{1,0:T(8,128)(2,1)S(1)}, bf16[128,1024]{1,0:T(8,128)(2,1)S(1)}, bf16[128,1024]{1,0:T(8,128)(2,1)S(1)}, f32[4,1024]{1,0:T(4,128)S(1)}) custom-call(bf16[128,1024]{1,0:T(8,128)(2,1)S(1)} %get-tuple-element.64.unit, f32[1,1024]{1,0:T(1,128)S(1)} %slice.120.g1, f32[1,1024]{1,0:T(1,128)S(1)} %slice.124.g2, ...), custom_call_target="tpu_custom_call" | custom-call | tf_op jit(solution)/shard_map/math_backward0/pallas_call | solution.py:525
  201.5 46.3 %exit.1 = (bf16[1024,256]{1,0:T(8,128)(2,1)S(1)}, bf16[1024,1024]{1,0:T(8,128)(2,1)S(1)}, bf16[1024,768]{1,0:T(8,128)(2,1)S(1)}, bf16[1024,1024]{1,0:T(8,128)(2,...) custom-call(bf16[128,256]{1,0:T(8,128)(2,1)S(1)} %copy-done.55, ...), custom_call_target="tpu_custom_call" | custom-call | tf_op jit(solution)/shard_map/exit/pallas_call | solution.py:537
  249.2 1.4 copy-done.20
  254.6 1.6 copy-done.17
  256.2 1.6 copy-done.19
  257.8 1.6 copy-done.21
  259.4 1.4 copy-done.32
  260.8 1.4 copy-done.34
  264.3 3.5 %math_grads.1 = (f32[2,128,768]{2,1,0:T(8,128)S(1)}, f32[2,256,128]{2,1,0:T(8,128)}, f32[2,128,1024]{2,1,0:T(8,128)}, f32[2,1024,128]{2,1,0:T(8,128)}, f32[2,768]{1,0:T(2,128)S(1)}, /*index=5*/f32[2,1024]{1,0:T(2,128)S(1)}) custom-call(bf16[8,2,2,128,128]{4,3,2,1,0:T(8,128)(2,1)S(1)} %get-tuple-element.100.cross, f32[2,4,128]{2,1,0:T(4,128)S(1)} %fusion.7.refs_0_, ...), custom_call_target="tpu_custom_call" | custom-call | tf_op jit(solution)/shard_map/math_grads/pallas_call | solution.py:525
  268.6 1.4 copy.116
  (273 shorter events, 79.9 us)
Async XLA Ops:
  0.6 56.5 %copy-start.93 = (s32[1,8]{1,0:T(1,128)S(1)}, s32[1,8]{1,0:T(1,128)}, u32[]{:S(2)}) copy-start(s32[1,8]{1,0:T(1,128)} %param.15) | copy-start | bytes 100
  59.6 1.6 copy-start.1
  69.5 108.2 %copy-start.54 = (bf16[128,256]{1,0:T(8,128)(2,1)}, bf16[128,256]{1,0:T(8,128)(2,1)S(1)}, u32[]{:S(2)}) copy-start(bf16[128,256]{1,0:T(8,128)(2,1)S(1)} %get-tuple-element.87.ctx.refs_0_) | copy-start | bytes 196612
  118.2 1.6 copy-start.4
  119.8 1.6 copy-start.7
  124.5 2.4 copy-start.5
  124.5 2.4 copy-start.13
  124.5 2.4 copy-start.41
  126.8 4.1 %copy-start.56 = (bf16[128,256]{1,0:T(8,128)(2,1)}, bf16[128,256]{1,0:T(8,128)(2,1)S(1)}, u32[]{:S(2)}) copy-start(bf16[128,256]{1,0:T(8,128)(2,1)S(1)} %get-tuple-element.76.ctx.refs_0_) | copy-start | bytes 196612
  126.8 4.1 %copy-start.67 = (bf16[128,1024]{1,0:T(8,128)(2,1)}, bf16[128,1024]{1,0:T(8,128)(2,1)S(1)}, u32[]{:S(2)}) copy-start(bf16[128,1024]{1,0:T(8,128)(2,1)S(1)} %get-tuple-element.77.refs_1_) | copy-start | bytes 786436
  126.9 4.1 %copy-start.69 = (bf16[128,1024]{1,0:T(8,128)(2,1)}, bf16[128,1024]{1,0:T(8,128)(2,1)S(1)}, u32[]{:S(2)}) copy-start(bf16[128,1024]{1,0:T(8,128)(2,1)S(1)} %get-tuple-element.85.refs_7_) | copy-start | bytes 786436
  126.9 6.8 %copy-start.92 = (f32[1,1,8,4,32]{4,1,0,2,3:T(1,128)S(1)}, f32[1,1,8,4,32]{4,1,0,2,3:T(1,128)}, u32[]{:S(2)}) copy-start(f32[1,1,8,4,32]{4,1,0,2,3:T(1,128)} %get-tuple-element.160) | copy-start | bytes 12292
  126.9 8.2 %copy-start.36 = (f32[32,1024]{1,0:T(8,128)S(1)}, f32[32,1024]{1,0:T(8,128)}, u32[]{:S(2)}) copy-start(f32[32,1024]{1,0:T(8,128)} %refs_6_.3) | copy-start | bytes 393220
  141.5 36.2 %copy-start.10 = (bf16[1024,768]{1,0:T(8,128)(2,1)S(1)}, bf16[1024,768]{1,0:T(8,128)(2,1)}, u32[]{:S(2)}) copy-start(bf16[1024,768]{1,0:T(8,128)(2,1)} %copy-done.8) | copy-start | bytes 4718596
  177.7 9.6 %copy-start.31 = (bf16[1024,768]{1,0:T(8,128)(2,1)}, bf16[1024,768]{1,0:T(8,128)(2,1)S(1)}, u32[]{:S(2)}) copy-start(bf16[1024,768]{1,0:T(8,128)(2,1)S(1)} %get-tuple-element.107.refs_7_) | copy-start | bytes 4718596
  177.7 9.6 %copy-start.42 = (bf16[128,1024]{1,0:T(8,128)(2,1)}, bf16[128,1024]{1,0:T(8,128)(2,1)S(1)}, u32[]{:S(2)}) copy-start(bf16[128,1024]{1,0:T(8,128)(2,1)S(1)} %get-tuple-element.89.d_rows) | copy-start | bytes 786436
  177.7 9.6 %copy-start.44 = (bf16[1024,256]{1,0:T(8,128)(2,1)}, bf16[1024,256]{1,0:T(8,128)(2,1)S(1)}, u32[]{:S(2)}) copy-start(bf16[1024,256]{1,0:T(8,128)(2,1)S(1)} %get-tuple-element.105.refs_5_) | copy-start | bytes 1572868
  177.7 9.6 %copy-start.50 = (f32[32,1024]{1,0:T(8,128)}, f32[32,1024]{1,0:T(8,128)S(1)}, u32[]{:S(2)}) copy-start(f32[32,1024]{1,0:T(8,128)S(1)} %get-tuple-element.95.refs_8_) | copy-start | bytes 393220
  177.8 9.6 %copy-start.83 = (f32[32,1024]{1,0:T(8,128)}, f32[32,1024]{1,0:T(8,128)S(1)}, u32[]{:S(2)}) copy-start(f32[32,1024]{1,0:T(8,128)S(1)} %get-tuple-element.198) | copy-start | bytes 393220
  177.8 2.5 copy-start.2
  195.7 58.9 %copy-start.15 = (bf16[1024,1024]{1,0:T(8,128)(2,1)S(1)}, bf16[1024,1024]{1,0:T(8,128)(2,1)}, u32[]{:S(2)}) copy-start(bf16[1024,1024]{1,0:T(8,128)(2,1)} %copy-done.14) | copy-start | bytes 6291460
  254.6 1.6 copy-start.17
  268.6 4.5 %copy-start.84 = (f32[32,1024]{1,0:T(8,128)S(1)}, f32[32,1024]{1,0:T(8,128)}, u32[]{:S(2)}) copy-start(f32[32,1024]{1,0:T(8,128)} %copy-done.83) | copy-start | bytes 393220
  268.6 5.2 %copy-start.86 = (f32[32,1024]{1,0:T(8,128)S(1)}, f32[32,1024]{1,0:T(8,128)}, u32[]{:S(2)}) copy-start(f32[32,1024]{1,0:T(8,128)} %copy-done.85) | copy-start | bytes 393220
  (70 other events, 68.1 us)
